TPU v7x, 512 devices: a whole 4x4x16 slice. The times are simulated.
512 devices in a mesh: seq: 64 (over z, y), head: 8 (over x, core).
Axes of the slice: x: 4, y: 4, z: 16, core: 2. Of those that a mesh axis runs over, the one named last changes fastest.
Arguments:
- tokens: bfloat16 [32768, 1024], P('seq', 'head'), may hold values from -6 to 6
- w_qkv: bfloat16 [1, 1024, 3, 1024], P(None, None, None, 'head'), may hold values from -0.1875 to 0.1875
- w_out: bfloat16 [1, 1024, 1024], P(None, 'head'), may hold values from -0.1875 to 0.1875
- gain_in: bfloat16 [1, 1024], replicated, may hold values from 0.099609375 to 1.8984375
- gain_mid: bfloat16 [1, 1024], P(None, 'head'), may hold values from 0.099609375 to 1.8984375
Outputs:
- hidden: bfloat16 [32768, 1024], P('seq', 'head')
All inputs are finite; a program needn't handle non-finite values.
Results may differ from a plain program's by a relative error of at most 0.014.
Values may be sent and summed in bfloat16 or wider, within the bound.
No kernel may reach another device: no remote copies, remote signals or barrier semaphores. Data moves between devices by JAX's collectives and lax.ppermute only.
A program may use at most 128 MiB of HBM per device.

v0:
```python
import math

import jax
import jax.numpy as jnp
import numpy as np
from jax import lax
from jax.sharding import PartitionSpec as P

D = 1024
H = 16
DH = 64


EPSILON = 1e-06
SQRT_TWO = math.sqrt(2.0)


def carried_in(shard, axis, join, neutral):
    place = lax.axis_index(axis)
    gathered = jax.tree.map(
        lambda a, kind: lax.all_gather(a.astype(kind), axis), shard, (jnp.bfloat16, jnp.bfloat16)
    )
    state = jax.tree.map(lambda a, e: jnp.zeros_like(a) + jnp.asarray(e, a.dtype), shard, neutral)

    def one(turn, state):
        return join(
            state,
            jax.tree.map(
                lambda a, own: lax.dynamic_index_in_dim(a, turn, 0, False).astype(own.dtype),
                gathered,
                shard,
            ),
        )

    return lax.fori_loop(0, place, one, state)


def expand(columns):
    width = columns.shape[1]
    first_ids, second_ids = np.triu_indices(width)
    factors = np.where(first_ids == second_ids, 1.0, SQRT_TWO).astype(np.float32)
    first_cols = jnp.take(columns, jnp.asarray(first_ids.astype(np.int32)), axis=1)
    second_cols = jnp.take(columns, jnp.asarray(second_ids.astype(np.int32)), axis=1)
    return jnp.asarray(factors)[None, :, None] * first_cols * second_cols


def add_pair(earlier, latter):
    return (earlier[0] + latter[0], earlier[1] + latter[1])


def shards(tokens, w_qkv, w_out, gain_in, gain_mid):
    hidden = tokens
    row_count = tokens.shape[0]
    local_heads = w_qkv.shape[3] // DH
    row_ids = jnp.arange(row_count, dtype=jnp.int32)
    causal = row_ids[:, None] >= row_ids[None, :]
    whole = lax.all_gather(hidden, "head", axis=1, tiled=True)
    wide = whole.astype(jnp.float32)
    normed = (
        wide
        * lax.rsqrt(jnp.mean(wide * wide, axis=1, keepdims=True) + EPSILON)
        * gain_in[0].astype(jnp.float32)
    ).astype(jnp.bfloat16)
    weight_heads = w_qkv[0].reshape(D, 3, local_heads, DH)
    projected = jnp.einsum(
        "td,dche->chet", normed, weight_heads, preferred_element_type=jnp.float32
    ).astype(jnp.bfloat16)
    query_cols = projected[0]
    key_cols = projected[1]
    value_cols = projected[2]
    key_feats = expand(key_cols.astype(jnp.float32)).astype(jnp.bfloat16)
    block_state = jnp.einsum(
        "hft,het->hfe", key_feats, value_cols, preferred_element_type=jnp.float32
    )
    block_norm = jnp.sum(key_feats, axis=2, dtype=jnp.float32)
    empty = (jnp.zeros_like(block_state), jnp.zeros_like(block_norm))
    prefix_state, prefix_norm = carried_in((block_state, block_norm), "seq", add_pair, empty)
    query_feats = (expand(query_cols.astype(jnp.float32)) / DH).astype(jnp.bfloat16)
    scores = jnp.einsum("hdt,hds->hts", query_cols, key_cols, preferred_element_type=jnp.float32)
    weights = jnp.where(causal[None], scores * scores / DH, 0.0)
    local_den = jnp.sum(weights, axis=2)
    local_num = jnp.einsum(
        "hts,hes->the", weights.astype(jnp.bfloat16), value_cols, preferred_element_type=jnp.float32
    )
    num_prefix = jnp.einsum(
        "hft,hfe->the",
        query_feats,
        prefix_state.astype(jnp.bfloat16),
        preferred_element_type=jnp.float32,
    )
    den_prefix = jnp.einsum(
        "hft,hf->th",
        query_feats,
        prefix_norm.astype(jnp.bfloat16),
        preferred_element_type=jnp.float32,
    )
    attended = (local_num + num_prefix) / (1.0 + local_den.T + den_prefix)[:, :, None]
    attended = attended.reshape(row_count, local_heads * DH)
    total_squares = lax.psum(jnp.sum(attended * attended, axis=1), "head")
    inverse_rms = lax.rsqrt(total_squares / (H * DH) + EPSILON)
    mixed_in = (attended * inverse_rms[:, None] * gain_mid[0].astype(jnp.float32)).astype(
        jnp.bfloat16
    )
    partial_out = jnp.dot(mixed_in, w_out[0], preferred_element_type=jnp.float32)
    update = lax.psum_scatter(
        partial_out.astype(jnp.bfloat16), "head", scatter_dimension=1, tiled=True
    ).astype(jnp.float32)
    hidden = (hidden.astype(jnp.float32) + update).astype(jnp.bfloat16)
    return hidden


def solution(mesh):
    placed = (
        P("seq", "head"),
        P(None, None, None, "head"),
        P(None, "head", None),
        P(),
        P(None, "head"),
    )
    return jax.shard_map(
        shards, mesh=mesh, in_specs=placed, out_specs=P("seq", "head"), check_vma=False
    )
```

profile of v0, /device:TPU:1, one launch (start us, length us, event | category | flops | bytes accessed | tf_op | source)
XLA Modules:
  0.0 746.1 jit_solution(16171810790137222430)
XLA Ops:
  6.5 0.0 copy-start
  6.5 0.0 all-gather.6.cloned.1.call-start
  6.5 0.7 all-gather.6.cloned.1.call-update
  7.3 0.0 all-gather.8.cloned.1.call-start
  7.3 1.4 copy.26
  8.7 0.7 mul.96
  9.4 0.7 pad_clamp_fusion.1
  10.1 0.7 pad_clamp_fusion
  10.8 35.3 %all-gather.6.cloned.1.call-done = bf16[512,1024]{1,0:T(8,128)(2,1)} async-done(((bf16[512,128]{1,0:T(8,128)(2,1)}), bf16[512,1024]{1,0:T(8,128)(2,1)}) %all-gather.6.cloned.1.call-update) | async-done | bytes 1048592 | tf_op jit(solution)/shard_map/all_gather | solution.py:57
  46.1 1.5 fusion.12
  47.6 1.9 fusion.18
  49.5 0.1 convert_bitcast_fusion
  49.6 0.0 copy-start.1
  49.6 0.2 copy.28
  49.8 13.7 %gather_fusion = f32[2080,2,512]{2,1,0:T(2,128)} fusion(f32[2,64,512]{2,0,1:T(2,128)S(1)} %copy.28, s32[3072]{0:T(1024)S(1)} %pad_clamp_fusion.1), kind=kCustom, calls=%fused_computation.clone | custom fusion | bytes 17047680 | tf_op jit(solution)/shard_map/jit(_take)/gather | solution.py:42
  63.6 0.0 copy-start.3
  63.6 13.7 %gather_fusion.1 = f32[2080,2,512]{2,1,0:T(2,128)} fusion(f32[2,64,512]{2,0,1:T(2,128)S(1)} %copy.28, s32[3072]{0:T(1024)S(1)} %pad_clamp_fusion), kind=kCustom, calls=%fused_computation.1.clone | custom fusion | bytes 17047680 | tf_op jit(solution)/shard_map/jit(_take)/gather | solution.py:43
  77.2 0.0 copy-done.3
  77.3 15.4 %fusion.28 = (bf16[2,2080]{0,1:T(8,128)(2,1)S(1)}, bf16[2,2080,512]{2,0,1:T(2,128)(2,1)S(1)}) fusion(f32[2080,2,512]{2,1,0:T(2,128)} %gather_fusion.1, f32[2080,2,512]{2,1,0:T(2,128)} %gather_fusion, f32[2080]{0:T(1024)S(1)} %copy-done.3), kind=kLoop, calls=%fused_computation.56 | loop fusion | flops 8515520 | bytes 21315840 | tf_op jit(solution)/shard_map/reduce_sum | solution.py:75
  92.7 0.0 copy-start.4
  92.7 2.2 fusion.9
  94.9 0.0 all-gather.8.cloned.1.call-update
  94.9 0.0 reduce-scatter.4.cloned.1.call-start
  95.0 0.0 copy-done.4
  95.0 0.1 reshape.49
  95.1 0.1 iota_compare_fusion
  95.2 0.2 copy.33
  95.4 13.7 %gather_fusion.2 = f32[2080,2,512]{2,1,0:T(2,128)} fusion(f32[2,64,512]{2,0,1:T(2,128)S(1)} %copy.33, s32[3072]{0:T(1024)S(1)} %pad_clamp_fusion.1), kind=kCustom, calls=%fused_computation.2.clone | custom fusion | bytes 17047680 | tf_op jit(solution)/shard_map/jit(_take)/gather | solution.py:42
  109.1 13.7 %gather_fusion.3 = f32[2080,2,512]{2,1,0:T(2,128)} fusion(f32[2,64,512]{2,0,1:T(2,128)S(1)} %copy.33, s32[3072]{0:T(1024)S(1)} %pad_clamp_fusion), kind=kCustom, calls=%fused_computation.3.clone | custom fusion | bytes 17047680 | tf_op jit(solution)/shard_map/jit(_take)/gather | solution.py:43
  122.8 0.2 copy.31
  123.0 92.5 %all-gather.2 = bf16[64,2,2080]{2,1,0:T(2,128)(2,1)} all-gather(bf16[1,2,2080]{2,1,0:T(2,128)(2,1)S(1)} %copy.31), channel_id=3, replica_groups=mesh['seq'=64,'head'=8] {'seq'}, dimensions={0}, use_global_device_ids=true | all-gather | bytes 540800 | tf_op jit(solution)/shard_map/all_gather | solution.py:21
  215.5 0.0 copy-done.1
  215.5 1.7 fusion.30
  217.2 10.5 %fusion.1 = bf16[2,2080,512]{2,0,1:T(2,128)(2,1)} fusion(f32[2080,2,512]{2,1,0:T(2,128)} %gather_fusion.3, f32[2080,2,512]{2,1,0:T(2,128)} %gather_fusion.2, f32[2080]{0:T(1024)S(1)} %copy-done.3), kind=kLoop, calls=%fused_computation.9 | loop fusion | flops 8519680 | bytes 21307520 | tf_op jit(solution)/shard_map/convert_element_type | solution.py:78
  227.7 173.8 %all-gather.8.cloned.1.call-done = bf16[128,2080,64]{1,2,0:T(8,128)(2,1)} async-done(((bf16[2,2080,64]{1,2,0:T(8,128)(2,1)}), bf16[128,2080,64]{1,2,0:T(8,128)(2,1)}) %all-gather.8.cloned.1.call-update) | async-done | bytes 34078736 | tf_op jit(solution)/shard_map/all_gather | solution.py:21
  401.5 0.1 broadcast_in_dim.39
  401.7 2.9 fusion.5
  404.6 0.0 copy-start.5
  404.6 3.2 fusion.7
  407.8 0.0 copy-start.2
  407.8 0.0 copy-done.5
  407.9 1.3 multiply_reduce_fusion
  409.1 13.2 %psum.7 = f32[512]{0:T(512)S(1)} all-reduce(f32[512]{0:T(512)S(1)} %get-tuple-element.78), channel_id=1, replica_groups=mesh['seq'=64,'head'=8] {'head'}, use_global_device_ids=true, to_apply=%region_6.8 | all-reduce | flops 512 | bytes 4096 | tf_op jit(solution)/shard_map/psum | solution.py:99
  422.3 0.1 multiply_convert_fusion
  422.4 0.0 copy-done
  422.4 0.5 convolution_convert_fusion
  422.9 1.3 copy.41
  424.2 0.0 reduce-scatter.4.cloned.1.call-update
  424.2 313.6 %reduce-scatter.4.cloned.1.call-done = bf16[128,512]{1,0:T(8,128)(2,1)} async-done(((bf16[1024,512]{1,0:T(8,128)(2,1)}), bf16[128,512]{1,0:T(8,128)(2,1)}) %reduce-scatter.4.cloned.1.call-update) | async-done | bytes 131088
  737.9 1.0 copy.42
  738.9 0.0 copy-done.2
  738.9 0.7 add_convert_fusion
  (8 shorter events, 0.1 us)
Async XLA Ops:
  6.5 415.9 %copy-start = (bf16[1,128,1024]{2,1,0:T(8,128)(2,1)S(1)}, bf16[1,128,1024]{2,1,0:T(8,128)(2,1)}, u32[]{:S(2)}) copy-start(bf16[1,128,1024]{2,1,0:T(8,128)(2,1)} %param.17) | copy-start | bytes 786436
  6.5 39.6 %all-gather.6.cloned.1.call-start = ((), (), s32[]{:S(2)}) async-start(), calls=%async_computation.1 | async-start | bytes 1179648 | tf_op jit(solution)/shard_map/all_gather | solution.py:57
  7.3 394.3 %all-gather.8.cloned.1.call-start = ((), (), s32[]{:S(2)}) async-start(), calls=%async_computation.2 | async-start | bytes 36208640 | tf_op jit(solution)/shard_map/all_gather | solution.py:21
  49.6 165.9 %copy-start.1 = (bf16[3,2,64,512]{3,2,1,0:T(8,128)(2,1)}, bf16[3,2,64,512]{3,2,1,0:T(8,128)(2,1)S(1)}, u32[]{:S(2)}) copy-start(bf16[3,2,64,512]{3,2,1,0:T(8,128)(2,1)S(1)} %convert_bitcast_fusion) | copy-start | bytes 1179652
  63.6 13.7 %copy-start.3 = (f32[2080]{0:T(1024)S(1)}, f32[2080]{0:T(1024)}, u32[]{:S(2)}) copy-start(f32[2080]{0:T(1024)} %constant.59.clone) | copy-start | bytes 24964
  92.7 2.3 copy-start.4
  94.9 642.9 %reduce-scatter.4.cloned.1.call-start = ((), (), s32[]{:S(2)}) async-start(), calls=%async_computation.3 | async-start | bytes 1179648
  404.6 3.2 copy-start.5
  407.8 331.1 %copy-start.2 = (bf16[512,128]{1,0:T(8,128)(2,1)S(1)}, bf16[512,128]{1,0:T(8,128)(2,1)}, u32[]{:S(2)}) copy-start(bf16[512,128]{1,0:T(8,128)(2,1)} %param.15) | copy-start | bytes 393220
Sparse Core Ops, SparseCore 0:
  9.4 36.5 all-gather.5
  95.1 306.4 all-gather.7
  424.4 313.4 reduce-scatter.3
where the time goes:
time: 754 us; the launch traced here: 746 us
  waiting for transfers between devices  523 us (69%)
  blocking collectives  106 us (14%)
  local copies, waits for them, and re-layouts  59.5 us (8%)
  other arithmetic  30.5 us (4%)
  matrix products  13.6 us (2%)
  between operations  13.3 us (2%)
    unnamed x4, waiting for transfers between devices  314 us
    all_gather x1, waiting for transfers between devices, carried_in(): lax.all_gather(a.astype(kind), axis)  174 us
    all_gather x1, blocking collectives, carried_in(): lax.all_gather(a.astype(kind), axis)  92.5 us
    all_gather x1, waiting for transfers between devices, shards(): whole = lax.all_gather(hidden, 'head', axis=1, tiled=True)  35.3 us
    gather x2, local copies, waits for them, and re-layouts, expand(): jnp.take(columns, jnp.asarray(first_ids.astype(np.int32)), axis=1)  27.4 us
    gather x2, local copies, waits for them, and re-layouts, expand(): jnp.take(columns, jnp.asarray(second_ids.astype(np.int32)), axis=1)  27.4 us
    reduce_sum x1, other arithmetic, shards(): block_norm = jnp.sum(key_feats, axis=2, dtype=jnp.float32)  15.4 us
  transfers between devices with their start and end apart: 3, of which 3 were waited for; matrix products, arithmetic and copies ran while one was open for 6% of the time, Pallas kernels for 0%

commit v1 on v0

v1 whole, which is shorter than its diff:
```python
import jax
import jax.numpy as jnp
from jax import lax
from jax.experimental import pallas as pl
from jax.experimental.pallas import tpu as pltpu
from jax.sharding import PartitionSpec as P

D = 1024
H = 16
DH = 64
T = 512
EPSILON = 1e-06
SHIFTS = 32
PLANE = 4
PLANES = 16
SLICE = 544
PIECE = 40
F32 = jnp.float32
BF16 = jnp.bfloat16
VMEM = pl.BlockSpec(memory_space=pltpu.VMEM)
SMEM = pl.BlockSpec(memory_space=pltpu.SMEM)
X_GROUPS = [[0, 2, 4, 6], [1, 3, 5, 7]]
Y_GROUPS = [[PLANE * z + y for y in range(PLANE)] for z in range(PLANES)]
Z_GROUPS = [[PLANE * z + y for z in range(PLANES)] for y in range(PLANE)]
CORE_SWAP = [(h, h ^ 1) for h in range(8)]


def dot(a, b):
    return jnp.dot(a, b, preferred_element_type=F32)


def call(kernel, outs, scratch=(), flops=0, moved=0, **kw):
    return pl.pallas_call(
        kernel,
        out_shape=outs,
        scratch_shapes=list(scratch),
        cost_estimate=pl.CostEstimate(flops=flops, bytes_accessed=moved, transcendentals=0),
        compiler_params=pltpu.CompilerParams(vmem_limit_bytes=40 * 1024 * 1024),
        **kw,
    )


def feature_rows(wide):
    base = wide.astype(BF16)
    for low in range(16):
        turned = (pltpu.roll(wide, DH - low, 0) if low else wide).astype(BF16)
        for high in range(3):
            shift = 16 * high + low
            if shift > SHIFTS:
                continue
            moved = turned
            if high:
                moved = jnp.concatenate([turned[16 * high :], turned[: 16 * high]], axis=0)
            yield shift, base * moved


def project_kernel(core, own, other, gain, weights, sent, q_t, k_nat, v_t, k_t, v_diag):
    c = core[0]
    for chunk in range(4):
        rows = pl.ds(128 * chunk, 128)
        total = jnp.zeros((128, 1), F32)
        for x in range(4):
            for part in (own, other):
                wide = part[x, rows, :].astype(F32)
                total += jnp.sum(wide * wide, axis=1, keepdims=True)
        inverse = lax.rsqrt(total / D + EPSILON)
        projected = jnp.zeros((128, 384), F32)
        for x in range(4):
            first, second = 2 * x + c, 2 * x + 1 - c
            left = (own[x, rows, :].astype(F32) * inverse * gain[pl.ds(first, 1), :]).astype(BF16)
            right = (other[x, rows, :].astype(F32) * inverse * gain[pl.ds(second, 1), :]).astype(BF16)
            both = jnp.concatenate(
                [
                    jnp.concatenate([weights[kind, block] for kind in range(3)], axis=1)
                    for block in (first, second)
                ],
                axis=0,
            )
            projected += dot(jnp.concatenate([left, right], axis=1), both)
        rounded = projected.astype(BF16)
        k_nat[rows, :] = rounded[:, 128:256]
        values = rounded[:, 256:384]
        lane = lax.broadcasted_iota(jnp.int32, values.shape, 1)
        v_diag[rows, :] = jnp.where(lane < DH, values, jnp.zeros_like(values))
        v_diag[pl.ds(T + 128 * chunk, 128), :] = jnp.where(lane >= DH, values, jnp.zeros_like(values))
        turned = rounded.astype(F32).T
        q_t[:, rows] = turned[0:128].astype(BF16)
        k_t[:, rows] = turned[128:256]
        v_t[:, rows] = turned[256:384].astype(BF16)
    right = v_diag[...]
    for (shift, first), (_, second) in zip(feature_rows(k_t[0:DH, :]), feature_rows(k_t[DH:, :])):
        state = dot(jnp.concatenate([first, second], axis=1), right).astype(BF16)
        if shift == SHIFTS:
            for y in range(PLANE):
                sent[y, 512:528, :] = state[16 * y : 16 * (y + 1)]
        else:
            sent[shift // 8, DH * (shift % 8) : DH * (shift % 8 + 1), :] = state
    gram = dot(k_t[...].astype(BF16), k_nat[...])
    lane = lax.broadcasted_iota(jnp.int32, (DH, 128), 1)
    gram = jnp.where(lane < DH, gram[0:DH], gram[DH:]).astype(BF16)
    for y in range(PLANE):
        sent[y, 528:544, :] = gram[16 * y : 16 * (y + 1)]


def merge_kernel(blocks, total):
    def summed(start, size):
        rows = slice(start, start + size)
        pairs = [blocks[y, rows, :].astype(F32) for y in range(PLANE)]
        return (pairs[0] + pairs[1]) + (pairs[2] + pairs[3])

    for z in range(PLANES):
        total[z, 0:32, :] = summed(32 * z, 32).astype(BF16)
    last, gram = summed(512, 16), summed(528, 16)
    row = lax.broadcasted_iota(jnp.int32, (PLANES, 8, 128), 1)
    extra = jnp.where(row == 0, last[:, None, :], jnp.where(row == 1, gram[:, None, :], 0.0))
    total[:, 32:40, :] = extra.astype(BF16)


def prefix_kernel(blocks, prefix):
    running = jnp.zeros((PIECE, 128), F32)
    for z in range(PLANES):
        prefix[z] = running.astype(BF16)
        if z < PLANES - 1:
            running += blocks[z].astype(F32)


def spread_kernel(prefix, blocks, out):
    def spread(running, start, size):
        rows = slice(start, start + size)
        for y in range(PLANE):
            out[y, rows, :] = running.astype(BF16)
            if y < PLANE - 1:
                running += blocks[y, rows, :].astype(F32)

    for z in range(PLANES):
        spread(prefix[z, 0:32, :].astype(F32), 32 * z, 32)
    extra = prefix[:, 32:40, :].astype(F32)
    spread(extra[:, 0, :], 512, 16)
    spread(extra[:, 1, :], 528, 16)


def local_kernel(q_t, k_nat, v_t, num, den):
    queries = q_t[...]
    row = lax.broadcasted_iota(jnp.int32, queries.shape, 0)
    for h in range(2):
        masked = jnp.where((row >= DH * h) & (row < DH * (h + 1)), queries, jnp.zeros_like(queries))
        for j in range(2):
            cols = slice(256 * j, 256 * (j + 1))
            total = jnp.zeros((DH, 256), F32)
            weight_sum = jnp.zeros((1, 256), F32)
            for i in range(j + 1):
                scores = dot(k_nat[256 * i : 256 * (i + 1), :], masked[:, cols])
                weights = scores * scores * (1.0 / DH)
                if i == j:
                    s_ids = lax.broadcasted_iota(jnp.int32, weights.shape, 0)
                    t_ids = lax.broadcasted_iota(jnp.int32, weights.shape, 1)
                    weights = jnp.where(s_ids <= t_ids, weights, 0.0)
                weight_sum += jnp.sum(weights, axis=0, keepdims=True)
                values = v_t[DH * h : DH * (h + 1), 256 * i : 256 * (i + 1)]
                total += dot(values, weights.astype(BF16))
            num[DH * h : DH * (h + 1), cols] = total
            den[h : h + 1, cols] = weight_sum
    den[2:8, :] = jnp.zeros((6, T), F32)


def finish_kernel(core, prefix, num, den, q_t, gain, weights, keep, give, feats):
    c = core[0]
    gram = jnp.concatenate([prefix[y, 528:544, :] for y in range(PLANE)], axis=0).astype(F32).T
    gram = gram.astype(BF16)
    dens = []
    for h in range(2):
        queries = q_t[DH * h : DH * (h + 1), :]
        wide = queries.astype(F32)
        both = dot(gram[DH * h : DH * (h + 1), :], queries)
        dens.append(jnp.sum(both * wide, axis=0, keepdims=True) * (1.0 / DH))
        for shift, product in feature_rows(wide):
            scale = (1.0 if shift in (0, SHIFTS) else 2.0) / DH
            feats[h, DH * shift : DH * (shift + 1), :] = product * jnp.asarray(scale, BF16)
    sums = [num[0:DH, :], num[DH:, :]]
    for group in range(9):
        if group < 8:
            state = prefix[group // 2, 256 * (group % 2) : 256 * (group % 2 + 1), :]
        else:
            state = jnp.concatenate([prefix[y, 512:528, :] for y in range(PLANE)], axis=0)
        turned = state.astype(F32).T.astype(BF16)
        rows = pl.ds(256 * group, 256 if group < 8 else DH)
        for h in range(2):
            sums[h] += dot(turned[DH * h : DH * (h + 1), :], feats[h, rows, :])
    attended = jnp.concatenate(
        [sums[h] / (1.0 + den[h : h + 1, :] + dens[h]) for h in range(2)], axis=0
    )
    squares = jnp.sum(attended * attended, axis=0, keepdims=True)
    column = jnp.broadcast_to(gain[...].astype(F32), (128, 128)).T
    mixed = jnp.concatenate(
        [attended[:, 128 * i : 128 * (i + 1)] * column for i in range(4)], axis=1
    ).astype(BF16)
    extra = split_rows(squares)
    for x in range(4):
        keep[x, 0:128, :] = dot(weights[2 * x + c], mixed).astype(BF16)
        give[x, 0:128, :] = dot(weights[2 * x + 1 - c], mixed).astype(BF16)
        keep[x, 128:136, :] = extra
        give[x, 128:136, :] = extra


def split_rows(squares):
    high = squares.astype(BF16).astype(F32)
    row = lax.broadcasted_iota(jnp.int32, (8, T), 0)
    return jnp.where(row == 0, high, jnp.where(row == 1, squares - high, 0.0)).astype(BF16)


def pair_kernel(keep, received, out):
    for x in range(4):
        out[x, 0:128, :] = (keep[x, 0:128, :].astype(F32) + received[x, 0:128, :].astype(F32)).astype(BF16)
        extra = keep[x, 128:136, :].astype(F32) + received[x, 128:136, :].astype(F32)
        out[x, 128:136, :] = split_rows(jnp.sum(extra, axis=0, keepdims=True))


def output_kernel(parts, hidden, out):
    total = parts[0, 0:128, :].astype(F32)
    extra = parts[0, 128:136, :].astype(F32)
    for x in range(1, 4):
        total += parts[x, 0:128, :].astype(F32)
        extra += parts[x, 128:136, :].astype(F32)
    squares = jnp.sum(extra, axis=0, keepdims=True)
    update = total * lax.rsqrt(squares / D + EPSILON)
    out[...] = (hidden[...].astype(F32) + update.T).astype(BF16)


def exchange(blocks, axis, groups):
    return lax.all_to_all(blocks, axis, 0, 0, axis_index_groups=groups)


def shards(tokens, w_qkv, w_out, gain_in, gain_mid):
    core = (lax.axis_index("head") & 1).astype(jnp.int32)[None]
    shape = jax.ShapeDtypeStruct
    weights = w_qkv[0].transpose(1, 0, 2).reshape(3, 8, 128, 128)
    gains = gain_in.reshape(8, 128).astype(F32)
    out_weights = w_out[0].reshape(128, 8, 128).transpose(1, 2, 0)
    own = exchange(jnp.broadcast_to(tokens, (4, T, 128)), "head", X_GROUPS)
    other = lax.ppermute(own, "head", CORE_SWAP)
    sent, q_t, k_nat, v_t = call(
        project_kernel,
        (
            shape((PLANE, SLICE, 128), BF16),
            shape((128, T), BF16),
            shape((T, 128), BF16),
            shape((128, T), BF16),
        ),
        scratch=[pltpu.VMEM((128, T), F32), pltpu.VMEM((2 * T, 128), BF16)],
        flops=2 * T * D * 384 + 2 * 2112 * T * 256,
        moved=3000000,
        in_specs=[SMEM, VMEM, VMEM, VMEM, VMEM],
        out_specs=(VMEM,) * 4,
    )(core, own, other, gains, weights)
    blocks = exchange(sent, "seq", Y_GROUPS)
    num, den = call(
        local_kernel,
        (shape((128, T), F32), shape((8, T), F32)),
        flops=2 * 2 * T * T * 128,
        moved=1000000,
        in_specs=[VMEM] * 3,
        out_specs=(VMEM,) * 2,
    )(q_t, k_nat, v_t)
    pieces = shape((PLANES, PIECE, 128), BF16)
    total = call(merge_kernel, pieces, moved=800000, in_specs=[VMEM], out_specs=VMEM)(blocks)
    received = exchange(total, "seq", Z_GROUPS)
    prefix = call(prefix_kernel, pieces, moved=400000, in_specs=[VMEM], out_specs=VMEM)(received)
    prefix = exchange(prefix, "seq", Z_GROUPS)
    spread = call(
        spread_kernel,
        shape((PLANE, SLICE, 128), BF16),
        moved=1300000,
        in_specs=[VMEM] * 2,
        out_specs=VMEM,
    )(prefix, blocks)
    spread = exchange(spread, "seq", Y_GROUPS)
    partial = shape((4, 136, T), BF16)
    keep, give = call(
        finish_kernel,
        (partial, partial),
        scratch=[pltpu.VMEM((2, 2112, T), BF16)],
        flops=2 * 2112 * T * 128,
        moved=2500000,
        in_specs=[SMEM] + [VMEM] * 6,
        out_specs=(VMEM,) * 2,
    )(core, spread, num, den, q_t, gain_mid, out_weights)
    received = lax.ppermute(give, "head", CORE_SWAP)
    paired = call(pair_kernel, partial, moved=1600000, in_specs=[VMEM] * 2, out_specs=VMEM)(
        keep, received
    )
    parts = exchange(paired, "head", X_GROUPS)
    return call(
        output_kernel,
        shape((T, 128), BF16),
        moved=900000,
        in_specs=[VMEM] * 2,
        out_specs=VMEM,
    )(parts, tokens)


def solution(mesh):
    placed = (
        P("seq", "head"),
        P(None, None, None, "head"),
        P(None, "head", None),
        P(),
        P(None, "head"),
    )
    return jax.shard_map(
        shards, mesh=mesh, in_specs=placed, out_specs=P("seq", "head"), check_vma=False
    )
```

time: 754 us -> 117 us (0.16); the launches traced: 746 us -> 117 us
  waiting for transfers between devices: 523 us -> 9.12 us
  local copies, waits for them, and re-layouts: 59.5 us -> 1.89 us
  other arithmetic: 30.5 us -> 0.01 us
  blocking collectives: 106 us -> 80 us
  starting transfers between devices: 0.08 us -> 19.1 us
  matrix products: 13.6 us -> 0 us
  between operations: 13.3 us -> 0.11 us
    unnamed x4 -> x0, waiting for transfers between devices: 314 us -> none
    all_gather x2 -> x0, waiting for transfers between devices: 209 us -> none  [the longest x1 174 us: carried_in(): lax.all_gather(a.astype(kind), axis)]
    all_gather x1 -> x0, blocking collectives: 92.5 us -> none  [carried_in(): lax.all_gather(a.astype(kind), axis)]
    all_to_all x0 -> x5, blocking collectives: none -> 80 us  [exchange(): return lax.all_to_all(blocks, axis, 0, 0, axis_index_groups=groups)]
    gather x4 -> x0, local copies, waits for them, and re-layouts: 54.8 us -> none  [the longest x2 27.4 us: expand(): jnp.take(columns, jnp.asarray(first_ids.astype(np.int32)), axis=1)]
    reduce_sum x2 -> x0, other arithmetic: 16.9 us -> none  [the longest x1 15.4 us: shards(): block_norm = jnp.sum(key_feats, axis=2, dtype=jnp.float32)]
    ppermute x0 -> x2, starting transfers between devices: none -> 15.5 us  [the longest x1 7.78 us: shards(): other = lax.ppermute(own, 'head', CORE_SWAP)]
    psum x1 -> x0, blocking collectives: 13.2 us -> none  [shards(): total_squares = lax.psum(jnp.sum(attended * attended, axis=1), 'head')]
  transfers between devices with their start and end apart: 3 -> 3, of which waited for: 3 -> 3; matrix products, arithmetic and copies ran while one was open for 6% -> 0% of each run, Pallas kernels for 0% -> 1%
where the time goes in v1:
time: 117 us
  blocking collectives  80 us (68%)
  starting transfers between devices  19.1 us (16%)
  waiting for transfers between devices  9.12 us (8%)
  Pallas kernels  6.56 us (6%)
  local copies, waits for them, and re-layouts  1.89 us (2%)
    all_to_all x5, blocking collectives, exchange(): return lax.all_to_all(blocks, axis, 0, 0, axis_index_groups=groups)  80 us
    ppermute x1, starting transfers between devices, shards(): other = lax.ppermute(own, 'head', CORE_SWAP)  7.78 us
    ppermute x1, starting transfers between devices, shards(): received = lax.ppermute(give, 'head', CORE_SWAP)  7.74 us
    all_to_all x1, waiting for transfers between devices, exchange(): return lax.all_to_all(blocks, axis, 0, 0, axis_index_groups=groups)  6.07 us
    all_to_all x1, starting transfers between devices, exchange(): return lax.all_to_all(blocks, axis, 0, 0, axis_index_groups=groups)  3.6 us
  transfers between devices with their start and end apart: 3, of which 3 were waited for; matrix products, arithmetic and copies ran while one was open for 0% of the time, Pallas kernels for 1%

profile of v1, /device:TPU:1, one launch (start us, length us, event | category | flops | bytes accessed | tf_op | source)
XLA Modules:
  0.0 116.8 jit_solution(1693050496991652447)
XLA Ops:
  0.0 0.0 copy-start.2
  0.0 1.0 broadcast_in_dim.7
  1.1 11.6 %all_to_all.30.own = bf16[4,512,128]{2,1,0:T(8,128)(2,1)S(1)} all-to-all(bf16[4,512,128]{2,1,0:T(8,128)(2,1)S(1)} %broadcast_in_dim.7), channel_id=1, replica_groups={{0,2,4,6},{1,3,5,7},{8,10,12,14},{9,11,13,15},{16,18,20,22},{17,19,21,2..., dimensions={0} | all-to-all | bytes 1048576 | tf_op jit(solution)/shard_map/all_to_all | solution.py:230
  12.6 0.0 copy-start.4
  12.6 7.8 %collective-permute-start = (bf16[4,512,128]{2,1,0:T(8,128)(2,1)S(1)}, bf16[4,512,128]{2,1,0:T(8,128)(2,1)S(1)}, u32[]{:S(2)}, u32[]{:S(2)}) collective-permute-start(bf16[4,512,128]{2,1,0:T(8,128)(2,1)S(1)} %all_to_all.30.own), channel_id=1, source_target_pairs={{0,1},{1,0},{2,3},{3,2},{4,5},{5,4},{6,7},{7,6},{8,9},{9,8},{10,11... | collective-permute-start | bytes 1572872 | tf_op jit(solution)/shard_map/ppermute | solution.py:240
  20.4 0.0 copy-done.4
  20.4 1.5 %collective-permute-done.other = bf16[4,512,128]{2,1,0:T(8,128)(2,1)S(1)} collective-permute-done((bf16[4,512,128]{2,1,0:T(8,128)(2,1)S(1)}, bf16[4,512,128]{2,1,0:T(8,128)(2,1)S(1)}, u32[]{:S(2)}, u32[]{:S(2)}) %collective-permute-start) | collective-permute-done | bytes 524320 | tf_op jit(solution)/shard_map/ppermute | solution.py:240
  21.9 0.0 copy-done.2
  21.9 2.3 %shard_map.55 = (bf16[4,544,128]{2,1,0:T(8,128)(2,1)S(1)}, bf16[128,512]{1,0:T(8,128)(2,1)S(1)}, bf16[512,128]{1,0:T(8,128)(2,1)S(1)}, bf16[128,512]{1,0:T(8,128)(2,1)S(1)}) custom-call(s32[1]{0:T(128)} %bitcast.core, bf16[4,512,128]{2,1,0:T(8,128)(2,1)S(1)} %all_to_all.30.own, bf16[4,512,128]{2,1,0:T(8,128)(2,1)S(1)} %collective-permute-done.other, ...), custom_call_target="tpu_custom_call" | custom-call | flops 956301312 | bytes 3000000 | tf_op jit(solution)/shard_map/pallas_call | solution.py:241
  24.2 11.8 %all_to_all.31.blocks = bf16[4,544,128]{2,1,0:T(8,128)(2,1)S(1)} all-to-all(bf16[4,544,128]{2,1,0:T(8,128)(2,1)S(1)} %get-tuple-element.13), channel_id=1, replica_groups={{0,8,16,24},{32,40,48,56},{64,72,80,88},{96,104,112,120},{128,136,144,1..., dimensions={0} | all-to-all | bytes 1114112 | tf_op jit(solution)/shard_map/all_to_all | solution.py:230
  36.0 0.1 shard_map.56
  36.1 26.0 %all_to_all.32.blocks = bf16[16,40,128]{2,1,0:T(8,128)(2,1)S(1)} all-to-all(bf16[16,40,128]{2,1,0:T(8,128)(2,1)S(1)} %shard_map.56), channel_id=1, replica_groups={{0,32,64,96,128,160,192,224,256,288,320,352,384,416,448,480},{8,40,72,1..., dimensions={0} | all-to-all | bytes 327680 | tf_op jit(solution)/shard_map/all_to_all | solution.py:230
  62.2 18.6 %all_to_all.33.prefix = bf16[16,40,128]{2,1,0:T(8,128)(2,1)S(1)} all-to-all(bf16[16,40,128]{2,1,0:T(8,128)(2,1)S(1)} %shard_map.57), channel_id=1, replica_groups={{0,32,64,96,128,160,192,224,256,288,320,352,384,416,448,480},{8,40,72,1..., dimensions={0} | all-to-all | bytes 327680 | tf_op jit(solution)/shard_map/all_to_all | solution.py:230
  80.8 0.9 shard_map.58
  81.7 0.0 copy-start.3
  81.7 3.6 %all-to-all-start.4 = ((bf16[4,544,128]{2,1,0:T(8,128)(2,1)}), bf16[4,544,128]{2,1,0:T(8,128)(2,1)S(1)}, u32[]{:S(2)}, u32[]{:S(2)}) async-start(bf16[4,544,128]{2,1,0:T(8,128)(2,1)} %shard_map.58), calls=%async_computation.4 | async-start | bytes 1114112 | tf_op jit(solution)/shard_map/all_to_all | solution.py:230
  85.3 0.0 copy-done.3
  85.3 0.2 copy.6
  85.5 0.8 shard_map.59
  86.3 6.1 %all-to-all-done.4.prefix = bf16[4,544,128]{2,1,0:T(8,128)(2,1)S(1)} async-done(((bf16[4,544,128]{2,1,0:T(8,128)(2,1)}), bf16[4,544,128]{2,1,0:T(8,128)(2,1)S(1)}, u32[]{:S(2)}, u32[]{:S(2)}) %all-to-all-start.4) | async-done | bytes 557088 | tf_op jit(solution)/shard_map/all_to_all | solution.py:230
  92.4 0.0 copy-start.1
  92.4 0.7 copy-done.1
  93.0 1.5 %shard_map.60 = (bf16[4,136,512]{2,1,0:T(8,128)(2,1)S(1)}, bf16[4,136,512]{2,1,0:T(8,128)(2,1)S(1)}) custom-call(s32[1]{0:T(128)} %bitcast.core, bf16[4,544,128]{2,1,0:T(8,128)(2,1)S(1)} %all-to-all-done.4.prefix, f32[128,512]{1,0:T(8,128)S(1)} %get-tuple-element.17.num, f32[8,512]{1,0:T(8,128)S(1)} %get-tuple-element.18.den, ...), custom_call_target="tpu_custom_call" | custom-call | flops 276824064 | bytes 2500000 | tf_op jit(solution)/shard_map/pallas_call | solution.py:278
  94.5 7.7 %collective-permute-start.1 = (bf16[4,136,512]{2,1,0:T(8,128)(2,1)S(1)}, bf16[4,136,512]{2,1,0:T(8,128)(2,1)S(1)}, u32[]{:S(2)}, u32[]{:S(2)}) collective-permute-start(bf16[4,136,512]{2,1,0:T(8,128)(2,1)S(1)} %get-tuple-element.20), channel_id=1, source_target_pairs={{0,1},{1,0},{2,3},{3,2},{4,5},{5,4},{6,7},{7,6},{8,9},{9,8},{10,11... | collective-permute-start | bytes 1671176 | tf_op jit(solution)/shard_map/ppermute | solution.py:287
  102.3 1.6 %collective-permute-done.1.received = bf16[4,136,512]{2,1,0:T(8,128)(2,1)S(1)} collective-permute-done((bf16[4,136,512]{2,1,0:T(8,128)(2,1)S(1)}, bf16[4,136,512]{2,1,0:T(8,128)(2,1)S(1)}, u32[]{:S(2)}, u32[]{:S(2)}) %collective-permute-start.1) | collective-permute-done | bytes 557088 | tf_op jit(solution)/shard_map/ppermute | solution.py:287
  103.8 0.2 shard_map.61
  104.0 0.0 copy-start
  104.0 12.0 %all_to_all.34.parts = bf16[4,136,512]{2,1,0:T(8,128)(2,1)S(1)} all-to-all(bf16[4,136,512]{2,1,0:T(8,128)(2,1)S(1)} %shard_map.61), channel_id=1, replica_groups={{0,2,4,6},{1,3,5,7},{8,10,12,14},{9,11,13,15},{16,18,20,22},{17,19,21,2..., dimensions={0} | all-to-all | bytes 1114112 | tf_op jit(solution)/shard_map/all_to_all | solution.py:230
  116.0 0.0 copy-done
  116.0 0.8 shard_map.62
  (2 shorter events, 0.0 us)
Async XLA Ops:
  0.0 21.9 %copy-start.2 = (bf16[1,1024,3,128]{3,1,2,0:T(8,128)(2,1)S(1)}, bf16[1,1024,3,128]{3,1,2,0:T(8,128)(2,1)}, u32[]{:S(2)}) copy-start(bf16[1,1024,3,128]{3,1,2,0:T(8,128)(2,1)} %param.6) | copy-start | bytes 2359300
  12.6 7.8 %copy-start.4 = (bf16[1,1024]{1,0:T(2,128)(2,1)S(1)}, bf16[1,1024]{1,0:T(2,128)(2,1)}, u32[]{:S(2)}) copy-start(bf16[1,1024]{1,0:T(2,128)(2,1)} %param.8) | copy-start | bytes 6148
  12.6 9.3 %collective-permute-start = (bf16[4,512,128]{2,1,0:T(8,128)(2,1)S(1)}, bf16[4,512,128]{2,1,0:T(8,128)(2,1)S(1)}, u32[]{:S(2)}, u32[]{:S(2)}) collective-permute-start(bf16[4,512,128]{2,1,0:T(8,128)(2,1)S(1)} %all_to_all.30.own), channel_id=1, source_target_pairs={{0,1},{1,0},{2,3},{3,2},{4,5},{5,4},{6,7},{7,6},{8,9},{9,8},{10,11... | collective-permute-start | bytes 1572872 | tf_op jit(solution)/shard_map/ppermute | solution.py:240
  81.7 3.6 %copy-start.3 = (bf16[1,128,1024]{2,1,0:T(8,128)(2,1)S(1)}, bf16[1,128,1024]{2,1,0:T(8,128)(2,1)}, u32[]{:S(2)}) copy-start(bf16[1,128,1024]{2,1,0:T(8,128)(2,1)} %param.7) | copy-start | bytes 786436
  81.7 10.7 %all-to-all-start.4 = ((bf16[4,544,128]{2,1,0:T(8,128)(2,1)}), bf16[4,544,128]{2,1,0:T(8,128)(2,1)S(1)}, u32[]{:S(2)}, u32[]{:S(2)}) async-start(bf16[4,544,128]{2,1,0:T(8,128)(2,1)} %shard_map.58), calls=%async_computation.4 | async-start | bytes 1114112 | tf_op jit(solution)/shard_map/all_to_all | solution.py:230
  92.4 0.7 copy-start.1
  94.5 9.3 %collective-permute-start.1 = (bf16[4,136,512]{2,1,0:T(8,128)(2,1)S(1)}, bf16[4,136,512]{2,1,0:T(8,128)(2,1)S(1)}, u32[]{:S(2)}, u32[]{:S(2)}) collective-permute-start(bf16[4,136,512]{2,1,0:T(8,128)(2,1)S(1)} %get-tuple-element.20), channel_id=1, source_target_pairs={{0,1},{1,0},{2,3},{3,2},{4,5},{5,4},{6,7},{7,6},{8,9},{9,8},{10,11... | collective-permute-start | bytes 1671176 | tf_op jit(solution)/shard_map/ppermute | solution.py:287
  104.0 12.0 %copy-start = (bf16[512,128]{1,0:T(8,128)(2,1)S(1)}, bf16[512,128]{1,0:T(8,128)(2,1)}, u32[]{:S(2)}) copy-start(bf16[512,128]{1,0:T(8,128)(2,1)} %hidden.1) | copy-start | bytes 393220

commit v2 on v1

--- a/solution.py
+++ b/solution.py
@@ -11,17 +11,19 @@
 T = 512
 EPSILON = 1e-06
 SHIFTS = 32
-PLANE = 4
-PLANES = 16
-SLICE = 544
+PLANE = 8
+PLANES = 8
+MAIN = 2048 // PLANE
+EDGE = DH // PLANE
+SLICE = MAIN + 2 * EDGE
 PIECE = 40
 F32 = jnp.float32
 BF16 = jnp.bfloat16
 VMEM = pl.BlockSpec(memory_space=pltpu.VMEM)
 SMEM = pl.BlockSpec(memory_space=pltpu.SMEM)
 X_GROUPS = [[0, 2, 4, 6], [1, 3, 5, 7]]
-Y_GROUPS = [[PLANE * z + y for y in range(PLANE)] for z in range(PLANES)]
-Z_GROUPS = [[PLANE * z + y for z in range(PLANES)] for y in range(PLANE)]
+NEAR_GROUPS = [[PLANE * z + y for y in range(PLANE)] for z in range(PLANES)]
+FAR_GROUPS = [[PLANE * z + y for z in range(PLANES)] for y in range(PLANE)]
 CORE_SWAP = [(h, h ^ 1) for h in range(8)]
 
 
@@ -92,25 +94,28 @@
         state = dot(jnp.concatenate([first, second], axis=1), right).astype(BF16)
         if shift == SHIFTS:
             for y in range(PLANE):
-                sent[y, 512:528, :] = state[16 * y : 16 * (y + 1)]
+                sent[y, MAIN : MAIN + EDGE, :] = state[EDGE * y : EDGE * (y + 1)]
         else:
-            sent[shift // 8, DH * (shift % 8) : DH * (shift % 8 + 1), :] = state
+            y, start = divmod(DH * shift, MAIN)
+            sent[y, start : start + DH, :] = state
     gram = dot(k_t[...].astype(BF16), k_nat[...])
     lane = lax.broadcasted_iota(jnp.int32, (DH, 128), 1)
     gram = jnp.where(lane < DH, gram[0:DH], gram[DH:]).astype(BF16)
     for y in range(PLANE):
-        sent[y, 528:544, :] = gram[16 * y : 16 * (y + 1)]
+        sent[y, MAIN + EDGE :, :] = gram[EDGE * y : EDGE * (y + 1)]
 
 
 def merge_kernel(blocks, total):
     def summed(start, size):
         rows = slice(start, start + size)
-        pairs = [blocks[y, rows, :].astype(F32) for y in range(PLANE)]
-        return (pairs[0] + pairs[1]) + (pairs[2] + pairs[3])
+        parts = [blocks[y, rows, :].astype(F32) for y in range(PLANE)]
+        while len(parts) > 1:
+            parts = [a + b for a, b in zip(parts[::2], parts[1::2])]
+        return parts[0]
 
     for z in range(PLANES):
         total[z, 0:32, :] = summed(32 * z, 32).astype(BF16)
-    last, gram = summed(512, 16), summed(528, 16)
+    last, gram = summed(MAIN, EDGE), summed(MAIN + EDGE, EDGE)
     row = lax.broadcasted_iota(jnp.int32, (PLANES, 8, 128), 1)
     extra = jnp.where(row == 0, last[:, None, :], jnp.where(row == 1, gram[:, None, :], 0.0))
     total[:, 32:40, :] = extra.astype(BF16)
@@ -135,11 +140,12 @@
     for z in range(PLANES):
         spread(prefix[z, 0:32, :].astype(F32), 32 * z, 32)
     extra = prefix[:, 32:40, :].astype(F32)
-    spread(extra[:, 0, :], 512, 16)
-    spread(extra[:, 1, :], 528, 16)
-
-
-def local_kernel(q_t, k_nat, v_t, num, den):
+    spread(extra[:, 0, :], MAIN, EDGE)
+    spread(extra[:, 1, :], MAIN + EDGE, EDGE)
+
+
+def local_kernel(q_t, k_nat, v_t, gain, num, den, column):
+    column[...] = jnp.broadcast_to(gain[...].astype(F32), (128, 128)).T
     queries = q_t[...]
     row = lax.broadcasted_iota(jnp.int32, queries.shape, 0)
     for h in range(2):
@@ -165,7 +171,7 @@
 
 def finish_kernel(core, prefix, num, den, q_t, gain, weights, keep, give, feats):
     c = core[0]
-    gram = jnp.concatenate([prefix[y, 528:544, :] for y in range(PLANE)], axis=0).astype(F32).T
+    gram = jnp.concatenate([prefix[y, MAIN + EDGE :, :] for y in range(PLANE)], axis=0).astype(F32).T
     gram = gram.astype(BF16)
     dens = []
     for h in range(2):
@@ -179,9 +185,10 @@
     sums = [num[0:DH, :], num[DH:, :]]
     for group in range(9):
         if group < 8:
-            state = prefix[group // 2, 256 * (group % 2) : 256 * (group % 2 + 1), :]
+            y, start = divmod(256 * group, MAIN)
+            state = prefix[y, start : start + 256, :]
         else:
-            state = jnp.concatenate([prefix[y, 512:528, :] for y in range(PLANE)], axis=0)
+            state = jnp.concatenate([prefix[y, MAIN : MAIN + EDGE, :] for y in range(PLANE)], axis=0)
         turned = state.astype(F32).T.astype(BF16)
         rows = pl.ds(256 * group, 256 if group < 8 else DH)
         for h in range(2):
@@ -190,7 +197,7 @@
         [sums[h] / (1.0 + den[h : h + 1, :] + dens[h]) for h in range(2)], axis=0
     )
     squares = jnp.sum(attended * attended, axis=0, keepdims=True)
-    column = jnp.broadcast_to(gain[...].astype(F32), (128, 128)).T
+    column = gain[...]
     mixed = jnp.concatenate(
         [attended[:, 128 * i : 128 * (i + 1)] * column for i in range(4)], axis=1
     ).astype(BF16)
@@ -252,20 +259,20 @@
         in_specs=[SMEM, VMEM, VMEM, VMEM, VMEM],
         out_specs=(VMEM,) * 4,
     )(core, own, other, gains, weights)
-    blocks = exchange(sent, "seq", Y_GROUPS)
-    num, den = call(
+    blocks = exchange(sent, "seq", NEAR_GROUPS)
+    num, den, gain = call(
         local_kernel,
-        (shape((128, T), F32), shape((8, T), F32)),
+        (shape((128, T), F32), shape((8, T), F32), shape((128, 128), F32)),
         flops=2 * 2 * T * T * 128,
         moved=1000000,
-        in_specs=[VMEM] * 3,
-        out_specs=(VMEM,) * 2,
-    )(q_t, k_nat, v_t)
+        in_specs=[VMEM] * 4,
+        out_specs=(VMEM,) * 3,
+    )(q_t, k_nat, v_t, gain_mid)
     pieces = shape((PLANES, PIECE, 128), BF16)
     total = call(merge_kernel, pieces, moved=800000, in_specs=[VMEM], out_specs=VMEM)(blocks)
-    received = exchange(total, "seq", Z_GROUPS)
+    received = exchange(total, "seq", FAR_GROUPS)
     prefix = call(prefix_kernel, pieces, moved=400000, in_specs=[VMEM], out_specs=VMEM)(received)
-    prefix = exchange(prefix, "seq", Z_GROUPS)
+    prefix = exchange(prefix, "seq", FAR_GROUPS)
     spread = call(
         spread_kernel,
         shape((PLANE, SLICE, 128), BF16),
@@ -273,7 +280,7 @@
         in_specs=[VMEM] * 2,
         out_specs=VMEM,
     )(prefix, blocks)
-    spread = exchange(spread, "seq", Y_GROUPS)
+    spread = exchange(spread, "seq", NEAR_GROUPS)
     partial = shape((4, 136, T), BF16)
     keep, give = call(
         finish_kernel,
@@ -283,7 +290,7 @@
         moved=2500000,
         in_specs=[SMEM] + [VMEM] * 6,
         out_specs=(VMEM,) * 2,
-    )(core, spread, num, den, q_t, gain_mid, out_weights)
+    )(core, spread, num, den, q_t, gain, out_weights)
     received = lax.ppermute(give, "head", CORE_SWAP)
     paired = call(pair_kernel, partial, moved=1600000, in_specs=[VMEM] * 2, out_specs=VMEM)(
         keep, received

time: 117 us -> 114 us (0.974)
  blocking collectives: 80 us -> 77.5 us
    all_to_all x5, blocking collectives: 80 us -> 77.5 us  [exchange(): return lax.all_to_all(blocks, axis, 0, 0, axis_index_groups=groups)]
where the time goes in v2:
time: 114 us; the launch traced here: 113 us
  blocking collectives  77.5 us (68%)
  starting transfers between devices  18.7 us (16%)
  waiting for transfers between devices  8.58 us (8%)
  Pallas kernels  6.54 us (6%)
  local copies, waits for them, and re-layouts  1.88 us (2%)
    all_to_all x5, blocking collectives, exchange(): return lax.all_to_all(blocks, axis, 0, 0, axis_index_groups=groups)  77.5 us
    ppermute x1, starting transfers between devices, shards(): other = lax.ppermute(own, 'head', CORE_SWAP)  7.78 us
    ppermute x1, starting transfers between devices, shards(): received = lax.ppermute(give, 'head', CORE_SWAP)  7.25 us
    all_to_all x1, waiting for transfers between devices, exchange(): return lax.all_to_all(blocks, axis, 0, 0, axis_index_groups=groups)  5.53 us
    all_to_all x1, starting transfers between devices, exchange(): return lax.all_to_all(blocks, axis, 0, 0, axis_index_groups=groups)  3.67 us
  transfers between devices with their start and end apart: 3, of which 3 were waited for; matrix products, arithmetic and copies ran while one was open for 0% of the time, Pallas kernels for 1%

profile of v2, /device:TPU:1, one launch (start us, length us, event | category | flops | bytes accessed | tf_op | source)
XLA Modules:
  0.0 113.4 jit_solution(5641079561607985264)
XLA Ops:
  0.0 0.0 copy-start.1
  0.0 1.0 broadcast_in_dim.7
  1.1 11.6 %all_to_all.30.own = bf16[4,512,128]{2,1,0:T(8,128)(2,1)S(1)} all-to-all(bf16[4,512,128]{2,1,0:T(8,128)(2,1)S(1)} %broadcast_in_dim.7), channel_id=1, replica_groups={{0,2,4,6},{1,3,5,7},{8,10,12,14},{9,11,13,15},{16,18,20,22},{17,19,21,2..., dimensions={0} | all-to-all | bytes 1048576 | tf_op jit(solution)/shard_map/all_to_all | solution.py:237
  12.6 0.0 copy-start.4
  12.6 7.8 %collective-permute-start = (bf16[4,512,128]{2,1,0:T(8,128)(2,1)S(1)}, bf16[4,512,128]{2,1,0:T(8,128)(2,1)S(1)}, u32[]{:S(2)}, u32[]{:S(2)}) collective-permute-start(bf16[4,512,128]{2,1,0:T(8,128)(2,1)S(1)} %all_to_all.30.own), channel_id=1, source_target_pairs={{0,1},{1,0},{2,3},{3,2},{4,5},{5,4},{6,7},{7,6},{8,9},{9,8},{10,11... | collective-permute-start | bytes 1572872 | tf_op jit(solution)/shard_map/ppermute | solution.py:247
  20.4 0.0 copy-done.4
  20.4 1.5 %collective-permute-done.other = bf16[4,512,128]{2,1,0:T(8,128)(2,1)S(1)} collective-permute-done((bf16[4,512,128]{2,1,0:T(8,128)(2,1)S(1)}, bf16[4,512,128]{2,1,0:T(8,128)(2,1)S(1)}, u32[]{:S(2)}, u32[]{:S(2)}) %collective-permute-start) | collective-permute-done | bytes 524320 | tf_op jit(solution)/shard_map/ppermute | solution.py:247
  21.9 0.0 copy-done.1
  21.9 2.3 %shard_map.55 = (bf16[8,272,128]{2,1,0:T(8,128)(2,1)S(1)}, bf16[128,512]{1,0:T(8,128)(2,1)S(1)}, bf16[512,128]{1,0:T(8,128)(2,1)S(1)}, bf16[128,512]{1,0:T(8,128)(2,1)S(1)}) custom-call(s32[1]{0:T(128)} %bitcast.core, bf16[4,512,128]{2,1,0:T(8,128)(2,1)S(1)} %all_to_all.30.own, bf16[4,512,128]{2,1,0:T(8,128)(2,1)S(1)} %collective-permute-done.other, ...), custom_call_target="tpu_custom_call" | custom-call | flops 956301312 | bytes 3000000 | tf_op jit(solution)/shard_map/pallas_call | solution.py:248
  24.2 13.1 %all_to_all.31.blocks = bf16[8,272,128]{2,1,0:T(8,128)(2,1)S(1)} all-to-all(bf16[8,272,128]{2,1,0:T(8,128)(2,1)S(1)} %get-tuple-element.14), channel_id=1, replica_groups={{0,8,16,24,32,40,48,56},{64,72,80,88,96,104,112,120},{128,136,144,152,1..., dimensions={0} | all-to-all | bytes 1114112 | tf_op jit(solution)/shard_map/all_to_all | solution.py:237
  37.3 0.1 shard_map.56
  37.4 26.1 %all_to_all.32.blocks = bf16[8,40,128]{2,1,0:T(8,128)(2,1)S(1)} all-to-all(bf16[8,40,128]{2,1,0:T(8,128)(2,1)S(1)} %shard_map.56), channel_id=1, replica_groups={{0,64,128,192,256,320,384,448},{8,72,136,200,264,328,392,456},{16,80,14..., dimensions={0} | all-to-all | bytes 163840 | tf_op jit(solution)/shard_map/all_to_all | solution.py:237
  63.5 14.8 %all_to_all.33.prefix = bf16[8,40,128]{2,1,0:T(8,128)(2,1)S(1)} all-to-all(bf16[8,40,128]{2,1,0:T(8,128)(2,1)S(1)} %shard_map.57), channel_id=1, replica_groups={{0,64,128,192,256,320,384,448},{8,72,136,200,264,328,392,456},{16,80,14..., dimensions={0} | all-to-all | bytes 163840 | tf_op jit(solution)/shard_map/all_to_all | solution.py:237
  78.3 0.9 shard_map.58
  79.2 0.0 copy-start.3
  79.2 3.7 %all-to-all-start.4 = ((bf16[8,272,128]{2,1,0:T(8,128)(2,1)}), bf16[8,272,128]{2,1,0:T(8,128)(2,1)S(1)}, u32[]{:S(2)}, u32[]{:S(2)}) async-start(bf16[8,272,128]{2,1,0:T(8,128)(2,1)} %shard_map.58), calls=%async_computation.4 | async-start | bytes 1114112 | tf_op jit(solution)/shard_map/all_to_all | solution.py:237
  82.9 0.0 copy-done.3
  82.9 0.2 copy.6
  83.1 0.0 copy-start.2
  83.1 0.6 copy-done.2
  83.7 0.8 shard_map.59
  84.6 5.5 %all-to-all-done.4.prefix = bf16[8,272,128]{2,1,0:T(8,128)(2,1)S(1)} async-done(((bf16[8,272,128]{2,1,0:T(8,128)(2,1)}), bf16[8,272,128]{2,1,0:T(8,128)(2,1)S(1)}, u32[]{:S(2)}, u32[]{:S(2)}) %all-to-all-start.4) | async-done | bytes 557088 | tf_op jit(solution)/shard_map/all_to_all | solution.py:237
  90.1 1.5 %shard_map.60 = (bf16[4,136,512]{2,1,0:T(8,128)(2,1)S(1)}, bf16[4,136,512]{2,1,0:T(8,128)(2,1)S(1)}) custom-call(s32[1]{0:T(128)} %bitcast.core, bf16[8,272,128]{2,1,0:T(8,128)(2,1)S(1)} %all-to-all-done.4.prefix, f32[128,512]{1,0:T(8,128)S(1)} %get-tuple-element.18.num, f32[8,512]{1,0:T(8,128)S(1)} %get-tuple-element.19.den, ...), custom_call_target="tpu_custom_call" | custom-call | flops 276824064 | bytes 2500000 | tf_op jit(solution)/shard_map/pallas_call | solution.py:285
  91.6 7.2 %collective-permute-start.1 = (bf16[4,136,512]{2,1,0:T(8,128)(2,1)S(1)}, bf16[4,136,512]{2,1,0:T(8,128)(2,1)S(1)}, u32[]{:S(2)}, u32[]{:S(2)}) collective-permute-start(bf16[4,136,512]{2,1,0:T(8,128)(2,1)S(1)} %get-tuple-element.22), channel_id=1, source_target_pairs={{0,1},{1,0},{2,3},{3,2},{4,5},{5,4},{6,7},{7,6},{8,9},{9,8},{10,11... | collective-permute-start | bytes 1671176 | tf_op jit(solution)/shard_map/ppermute | solution.py:294
  98.8 1.6 %collective-permute-done.1.received = bf16[4,136,512]{2,1,0:T(8,128)(2,1)S(1)} collective-permute-done((bf16[4,136,512]{2,1,0:T(8,128)(2,1)S(1)}, bf16[4,136,512]{2,1,0:T(8,128)(2,1)S(1)}, u32[]{:S(2)}, u32[]{:S(2)}) %collective-permute-start.1) | collective-permute-done | bytes 557088 | tf_op jit(solution)/shard_map/ppermute | solution.py:294
  100.4 0.2 shard_map.61
  100.6 0.0 copy-start
  100.6 12.0 %all_to_all.34.parts = bf16[4,136,512]{2,1,0:T(8,128)(2,1)S(1)} all-to-all(bf16[4,136,512]{2,1,0:T(8,128)(2,1)S(1)} %shard_map.61), channel_id=1, replica_groups={{0,2,4,6},{1,3,5,7},{8,10,12,14},{9,11,13,15},{16,18,20,22},{17,19,21,2..., dimensions={0} | all-to-all | bytes 1114112 | tf_op jit(solution)/shard_map/all_to_all | solution.py:237
  112.6 0.0 copy-done
  112.6 0.8 shard_map.62
  (2 shorter events, 0.0 us)
Async XLA Ops:
  0.0 21.9 %copy-start.1 = (bf16[1,1024,3,128]{3,1,2,0:T(8,128)(2,1)S(1)}, bf16[1,1024,3,128]{3,1,2,0:T(8,128)(2,1)}, u32[]{:S(2)}) copy-start(bf16[1,1024,3,128]{3,1,2,0:T(8,128)(2,1)} %param.6) | copy-start | bytes 2359300
  12.6 7.8 %copy-start.4 = (bf16[1,1024]{1,0:T(2,128)(2,1)S(1)}, bf16[1,1024]{1,0:T(2,128)(2,1)}, u32[]{:S(2)}) copy-start(bf16[1,1024]{1,0:T(2,128)(2,1)} %param.8) | copy-start | bytes 6148
  12.6 9.3 %collective-permute-start = (bf16[4,512,128]{2,1,0:T(8,128)(2,1)S(1)}, bf16[4,512,128]{2,1,0:T(8,128)(2,1)S(1)}, u32[]{:S(2)}, u32[]{:S(2)}) collective-permute-start(bf16[4,512,128]{2,1,0:T(8,128)(2,1)S(1)} %all_to_all.30.own), channel_id=1, source_target_pairs={{0,1},{1,0},{2,3},{3,2},{4,5},{5,4},{6,7},{7,6},{8,9},{9,8},{10,11... | collective-permute-start | bytes 1572872 | tf_op jit(solution)/shard_map/ppermute | solution.py:247
  79.2 3.7 %copy-start.3 = (bf16[1,128,1024]{2,1,0:T(8,128)(2,1)S(1)}, bf16[1,128,1024]{2,1,0:T(8,128)(2,1)}, u32[]{:S(2)}) copy-start(bf16[1,128,1024]{2,1,0:T(8,128)(2,1)} %param.7) | copy-start | bytes 786436
  79.2 10.9 %all-to-all-start.4 = ((bf16[8,272,128]{2,1,0:T(8,128)(2,1)}), bf16[8,272,128]{2,1,0:T(8,128)(2,1)S(1)}, u32[]{:S(2)}, u32[]{:S(2)}) async-start(bf16[8,272,128]{2,1,0:T(8,128)(2,1)} %shard_map.58), calls=%async_computation.4 | async-start | bytes 1114112 | tf_op jit(solution)/shard_map/all_to_all | solution.py:237
  83.1 0.7 copy-start.2
  91.6 8.8 %collective-permute-start.1 = (bf16[4,136,512]{2,1,0:T(8,128)(2,1)S(1)}, bf16[4,136,512]{2,1,0:T(8,128)(2,1)S(1)}, u32[]{:S(2)}, u32[]{:S(2)}) collective-permute-start(bf16[4,136,512]{2,1,0:T(8,128)(2,1)S(1)} %get-tuple-element.22), channel_id=1, source_target_pairs={{0,1},{1,0},{2,3},{3,2},{4,5},{5,4},{6,7},{7,6},{8,9},{9,8},{10,11... | collective-permute-start | bytes 1671176 | tf_op jit(solution)/shard_map/ppermute | solution.py:294
  100.6 12.0 %copy-start = (bf16[512,128]{1,0:T(8,128)(2,1)S(1)}, bf16[512,128]{1,0:T(8,128)(2,1)}, u32[]{:S(2)}) copy-start(bf16[512,128]{1,0:T(8,128)(2,1)} %hidden.1) | copy-start | bytes 393220

commit v3 on v2

--- a/solution.py
+++ b/solution.py
@@ -11,12 +11,11 @@
 T = 512
 EPSILON = 1e-06
 SHIFTS = 32
-PLANE = 8
-PLANES = 8
+PLANE = 16
+PLANES = 4
 MAIN = 2048 // PLANE
 EDGE = DH // PLANE
 SLICE = MAIN + 2 * EDGE
-PIECE = 40
 F32 = jnp.float32
 BF16 = jnp.bfloat16
 VMEM = pl.BlockSpec(memory_space=pltpu.VMEM)
@@ -90,58 +89,44 @@
         k_t[:, rows] = turned[128:256]
         v_t[:, rows] = turned[256:384].astype(BF16)
     right = v_diag[...]
+    last = None
     for (shift, first), (_, second) in zip(feature_rows(k_t[0:DH, :]), feature_rows(k_t[DH:, :])):
         state = dot(jnp.concatenate([first, second], axis=1), right).astype(BF16)
         if shift == SHIFTS:
-            for y in range(PLANE):
-                sent[y, MAIN : MAIN + EDGE, :] = state[EDGE * y : EDGE * (y + 1)]
+            last = state
         else:
             y, start = divmod(DH * shift, MAIN)
             sent[y, start : start + DH, :] = state
     gram = dot(k_t[...].astype(BF16), k_nat[...])
     lane = lax.broadcasted_iota(jnp.int32, (DH, 128), 1)
     gram = jnp.where(lane < DH, gram[0:DH], gram[DH:]).astype(BF16)
+    edge = dot(edge_rows(128, DH, 0), last) + dot(edge_rows(128, DH, EDGE), gram)
+    sent[:, MAIN:, :] = edge.astype(BF16).reshape(PLANE, 2 * EDGE, 128)
+
+
+def edge_rows(rows, columns, offset):
+    row = lax.broadcasted_iota(jnp.int32, (rows, columns), 0)
+    column = lax.broadcasted_iota(jnp.int32, (rows, columns), 1)
+    place, a = (row, column) if rows == 128 else (column, row)
+    hit = place == 2 * EDGE * (a // EDGE) + a % EDGE + offset
+    return jnp.where(hit, 1.0, 0.0).astype(BF16)
+
+
+def merge_kernel(blocks, total):
+    parts = [blocks[y].astype(F32) for y in range(PLANE)]
+    while len(parts) > 1:
+        parts = [a + b for a, b in zip(parts[::2], parts[1::2])]
+    total[...] = parts[0].astype(BF16)
+
+
+def spread_kernel(first, second, third, fourth, blocks, out):
+    running = (first[...].astype(F32) + second[...].astype(F32)) + (
+        third[...].astype(F32) + fourth[...].astype(F32)
+    )
     for y in range(PLANE):
-        sent[y, MAIN + EDGE :, :] = gram[EDGE * y : EDGE * (y + 1)]
-
-
-def merge_kernel(blocks, total):
-    def summed(start, size):
-        rows = slice(start, start + size)
-        parts = [blocks[y, rows, :].astype(F32) for y in range(PLANE)]
-        while len(parts) > 1:
-            parts = [a + b for a, b in zip(parts[::2], parts[1::2])]
-        return parts[0]
-
-    for z in range(PLANES):
-        total[z, 0:32, :] = summed(32 * z, 32).astype(BF16)
-    last, gram = summed(MAIN, EDGE), summed(MAIN + EDGE, EDGE)
-    row = lax.broadcasted_iota(jnp.int32, (PLANES, 8, 128), 1)
-    extra = jnp.where(row == 0, last[:, None, :], jnp.where(row == 1, gram[:, None, :], 0.0))
-    total[:, 32:40, :] = extra.astype(BF16)
-
-
-def prefix_kernel(blocks, prefix):
-    running = jnp.zeros((PIECE, 128), F32)
-    for z in range(PLANES):
-        prefix[z] = running.astype(BF16)
-        if z < PLANES - 1:
-            running += blocks[z].astype(F32)
-
-
-def spread_kernel(prefix, blocks, out):
-    def spread(running, start, size):
-        rows = slice(start, start + size)
-        for y in range(PLANE):
-            out[y, rows, :] = running.astype(BF16)
-            if y < PLANE - 1:
-                running += blocks[y, rows, :].astype(F32)
-
-    for z in range(PLANES):
-        spread(prefix[z, 0:32, :].astype(F32), 32 * z, 32)
-    extra = prefix[:, 32:40, :].astype(F32)
-    spread(extra[:, 0, :], MAIN, EDGE)
-    spread(extra[:, 1, :], MAIN + EDGE, EDGE)
+        out[y] = running.astype(BF16)
+        if y < PLANE - 1:
+            running += blocks[y].astype(F32)
 
 
 def local_kernel(q_t, k_nat, v_t, gain, num, den, column):
@@ -171,8 +156,8 @@
 
 def finish_kernel(core, prefix, num, den, q_t, gain, weights, keep, give, feats):
     c = core[0]
-    gram = jnp.concatenate([prefix[y, MAIN + EDGE :, :] for y in range(PLANE)], axis=0).astype(F32).T
-    gram = gram.astype(BF16)
+    edge = prefix[:, MAIN:, :].reshape(128, 128)
+    gram = dot(edge_rows(DH, 128, EDGE), edge).T.astype(BF16)
     dens = []
     for h in range(2):
         queries = q_t[DH * h : DH * (h + 1), :]
@@ -185,10 +170,9 @@
     sums = [num[0:DH, :], num[DH:, :]]
     for group in range(9):
         if group < 8:
-            y, start = divmod(256 * group, MAIN)
-            state = prefix[y, start : start + 256, :]
+            state = jnp.concatenate([prefix[2 * group, 0:MAIN, :], prefix[2 * group + 1, 0:MAIN, :]], axis=0)
         else:
-            state = jnp.concatenate([prefix[y, MAIN : MAIN + EDGE, :] for y in range(PLANE)], axis=0)
+            state = dot(edge_rows(DH, 128, 0), edge)
         turned = state.astype(F32).T.astype(BF16)
         rows = pl.ds(256 * group, 256 if group < 8 else DH)
         for h in range(2):
@@ -235,6 +219,12 @@
 
 def exchange(blocks, axis, groups):
     return lax.all_to_all(blocks, axis, 0, 0, axis_index_groups=groups)
+
+
+def forward(total, pairs):
+    return lax.ppermute(
+        total, "seq", [(PLANE * a + i, PLANE * b + i) for a, b in pairs for i in range(PLANE)]
+    )
 
 
 def shards(tokens, w_qkv, w_out, gain_in, gain_mid):
@@ -268,18 +258,23 @@
         in_specs=[VMEM] * 4,
         out_specs=(VMEM,) * 3,
     )(q_t, k_nat, v_t, gain_mid)
-    pieces = shape((PLANES, PIECE, 128), BF16)
-    total = call(merge_kernel, pieces, moved=800000, in_specs=[VMEM], out_specs=VMEM)(blocks)
-    received = exchange(total, "seq", FAR_GROUPS)
-    prefix = call(prefix_kernel, pieces, moved=400000, in_specs=[VMEM], out_specs=VMEM)(received)
-    prefix = exchange(prefix, "seq", FAR_GROUPS)
+    total = call(
+        merge_kernel,
+        shape((SLICE, 128), BF16),
+        moved=800000,
+        in_specs=[VMEM],
+        out_specs=VMEM,
+    )(blocks)
+    direct = forward(total, ((0, 1), (2, 3)))
+    earlier = [direct, forward(total, ((0, 3),)), forward(total, ((1, 3),))]
+    earlier.append(forward(total + direct, ((1, 2),)))
     spread = call(
         spread_kernel,
         shape((PLANE, SLICE, 128), BF16),
         moved=1300000,
-        in_specs=[VMEM] * 2,
+        in_specs=[VMEM] * 5,
         out_specs=VMEM,
-    )(prefix, blocks)
+    )(*earlier, blocks)
     spread = exchange(spread, "seq", NEAR_GROUPS)
     partial = shape((4, 136, T), BF16)
     keep, give = call(

time: 114 us -> 101 us (0.89)
  blocking collectives: 77.5 us -> 45.9 us
  starting transfers between devices: 18.7 us -> 32.1 us
  waiting for transfers between devices: 8.58 us -> 13.7 us
    all_to_all x5 -> x3, blocking collectives: 77.5 us -> 45.9 us  [exchange(): return lax.all_to_all(blocks, axis, 0, 0, axis_index_groups=groups)]
    ppermute x0 -> x4, starting transfers between devices: none -> 13 us  [forward(): lax.ppermute(total, 'seq', [(PLANE * a + i, PLANE * b + i) for a, b in pa...]
    all_to_all x1, waiting for transfers between devices: 5.53 us -> 10.3 us  [exchange(): return lax.all_to_all(blocks, axis, 0, 0, axis_index_groups=groups)]
  transfers between devices with their start and end apart: 3 -> 7, of which waited for: 3 -> 4; matrix products, arithmetic and copies ran while one was open for 0% -> 0% of each run, Pallas kernels for 1% -> 1%
where the time goes in v3:
time: 101 us
  blocking collectives  45.9 us (45%)
  starting transfers between devices  32.1 us (32%)
  waiting for transfers between devices  13.7 us (14%)
  Pallas kernels  7.03 us (7%)
  local copies, waits for them, and re-layouts  1.88 us (2%)
    all_to_all x3, blocking collectives, exchange(): return lax.all_to_all(blocks, axis, 0, 0, axis_index_groups=groups)  45.9 us
    ppermute x4, starting transfers between devices, forward(): lax.ppermute(total, 'seq', [(PLANE * a + i, PLANE * b + i) for a, b in pa...  13 us
    all_to_all x1, waiting for transfers between devices, exchange(): return lax.all_to_all(blocks, axis, 0, 0, axis_index_groups=groups)  10.3 us
    ppermute x1, starting transfers between devices, shards(): other = lax.ppermute(own, 'head', CORE_SWAP)  7.78 us
    ppermute x1, starting transfers between devices, shards(): received = lax.ppermute(give, 'head', CORE_SWAP)  6.99 us
    all_to_all x1, starting transfers between devices, exchange(): return lax.all_to_all(blocks, axis, 0, 0, axis_index_groups=groups)  4.3 us
    pallas_call x1, Pallas kernels, shards(): call(project_kernel, (shape((PLANE, SLICE, 128), BF16), shape((128, T), B...  2.46 us
  transfers between devices with their start and end apart: 7, of which 4 were waited for; matrix products, arithmetic and copies ran while one was open for 0% of the time, Pallas kernels for 1%

profile of v3, /device:TPU:1, one launch (start us, length us, event | category | flops | bytes accessed | tf_op | source)
XLA Modules:
  0.0 100.8 jit_solution(15938055213316584921)
XLA Ops:
  0.0 0.0 copy-start.1
  0.0 1.0 %broadcast_in_dim.7 = bf16[4,512,128]{2,1,0:T(8,128)(2,1)S(1)} broadcast(bf16[512,128]{1,0:T(8,128)(2,1)} %hidden.1), dimensions={1,2} | broadcast | bytes 655360 | tf_op jit(solution)/shard_map/broadcast_in_dim | solution.py:236
  1.1 11.6 %all_to_all.20.own = bf16[4,512,128]{2,1,0:T(8,128)(2,1)S(1)} all-to-all(bf16[4,512,128]{2,1,0:T(8,128)(2,1)S(1)} %broadcast_in_dim.7), channel_id=1, replica_groups={{0,2,4,6},{1,3,5,7},{8,10,12,14},{9,11,13,15},{16,18,20,22},{17,19,21,2..., dimensions={0} | all-to-all | bytes 1048576 | tf_op jit(solution)/shard_map/all_to_all | solution.py:221
  12.6 0.0 copy-start.4
  12.6 7.8 %collective-permute-start = (bf16[4,512,128]{2,1,0:T(8,128)(2,1)S(1)}, bf16[4,512,128]{2,1,0:T(8,128)(2,1)S(1)}, u32[]{:S(2)}, u32[]{:S(2)}) collective-permute-start(bf16[4,512,128]{2,1,0:T(8,128)(2,1)S(1)} %all_to_all.20.own), channel_id=1, source_target_pairs={{0,1},{1,0},{2,3},{3,2},{4,5},{5,4},{6,7},{7,6},{8,9},{9,8},{10,11... | collective-permute-start | bytes 1572872 | tf_op jit(solution)/shard_map/ppermute | solution.py:237
  20.4 0.0 copy-done.4
  20.4 1.5 %collective-permute-done.other = bf16[4,512,128]{2,1,0:T(8,128)(2,1)S(1)} collective-permute-done((bf16[4,512,128]{2,1,0:T(8,128)(2,1)S(1)}, bf16[4,512,128]{2,1,0:T(8,128)(2,1)S(1)}, u32[]{:S(2)}, u32[]{:S(2)}) %collective-permute-start) | collective-permute-done | bytes 524320 | tf_op jit(solution)/shard_map/ppermute | solution.py:237
  21.9 0.0 copy-done.1
  21.9 2.5 %shard_map.55 = (bf16[16,136,128]{2,1,0:T(8,128)(2,1)S(1)}, bf16[128,512]{1,0:T(8,128)(2,1)S(1)}, bf16[512,128]{1,0:T(8,128)(2,1)S(1)}, bf16[128,512]{1,0:T(8,128)(2,1)S(1)}) custom-call(s32[1]{0:T(128)} %bitcast.core, bf16[4,512,128]{2,1,0:T(8,128)(2,1)S(1)} %all_to_all.20.own, bf16[4,512,128]{2,1,0:T(8,128)(2,1)S(1)} %collective-permute-done.other, ...), custom_call_target="tpu_custom_call" | custom-call | flops 956301312 | bytes 3000000 | tf_op jit(solution)/shard_map/pallas_call | solution.py:238
  24.4 22.4 %all_to_all.21.blocks = bf16[16,136,128]{2,1,0:T(8,128)(2,1)S(1)} all-to-all(bf16[16,136,128]{2,1,0:T(8,128)(2,1)S(1)} %get-tuple-element.14), channel_id=1, replica_groups={{0,8,16,24,32,40,48,56,64,72,80,88,96,104,112,120},{128,136,144,152,160..., dimensions={0} | all-to-all | bytes 1114112 | tf_op jit(solution)/shard_map/all_to_all | solution.py:221
  46.7 0.1 shard_map.56
  46.8 8.8 %collective-permute-start.1 = (bf16[136,128]{1,0:T(8,128)(2,1)S(1)}, bf16[136,128]{1,0:T(8,128)(2,1)S(1)}, u32[]{:S(2)}, u32[]{:S(2)}) collective-permute-start(bf16[136,128]{1,0:T(8,128)(2,1)S(1)} %shard_map.56), channel_id=1, source_target_pairs={{0,128},{8,136},{16,144},{24,152},{32,160},{40,168},{48,176},{56,1... | collective-permute-start | bytes 104456 | tf_op jit(solution)/shard_map/ppermute | solution.py:225
  55.6 0.7 collective-permute-start.3
  56.3 2.9 %collective-permute-start.2 = (bf16[136,128]{1,0:T(8,128)(2,1)S(1)}, bf16[136,128]{1,0:T(8,128)(2,1)S(1)}, u32[]{:S(2)}, u32[]{:S(2)}) collective-permute-start(bf16[136,128]{1,0:T(8,128)(2,1)S(1)} %shard_map.56), channel_id=1, source_target_pairs={{0,384},{8,392},{16,400},{24,408},{32,416},{40,424},{48,432},{56,4... | collective-permute-start | bytes 104456 | tf_op jit(solution)/shard_map/ppermute | solution.py:225
  59.2 0.0 collective-permute-done.1.first
  59.2 0.7 collective-permute-start.4
  59.9 0.0 collective-permute-done.3.third
  59.9 0.3 collective-permute-done.2.second
  60.2 0.0 collective-permute-done.4.fourth
  60.2 0.9 shard_map.57
  61.1 0.0 copy-start.3
  61.1 4.3 %all-to-all-start.2 = ((bf16[16,136,128]{2,1,0:T(8,128)(2,1)}), bf16[16,136,128]{2,1,0:T(8,128)(2,1)S(1)}, u32[]{:S(2)}, u32[]{:S(2)}) async-start(bf16[16,136,128]{2,1,0:T(8,128)(2,1)} %shard_map.57), calls=%async_computation.2 | async-start | bytes 1114112 | tf_op jit(solution)/shard_map/all_to_all | solution.py:221
  65.4 0.0 copy-done.3
  65.4 0.2 copy.6
  65.6 0.0 copy-start.2
  65.6 0.6 copy-done.2
  66.3 0.8 shard_map.58
  67.1 10.3 %all-to-all-done.2.prefix = bf16[16,136,128]{2,1,0:T(8,128)(2,1)S(1)} async-done(((bf16[16,136,128]{2,1,0:T(8,128)(2,1)}), bf16[16,136,128]{2,1,0:T(8,128)(2,1)S(1)}, u32[]{:S(2)}, u32[]{:S(2)}) %all-to-all-start.2) | async-done | bytes 557088 | tf_op jit(solution)/shard_map/all_to_all | solution.py:221
  77.4 1.8 %shard_map.59 = (bf16[4,136,512]{2,1,0:T(8,128)(2,1)S(1)}, bf16[4,136,512]{2,1,0:T(8,128)(2,1)S(1)}) custom-call(s32[1]{0:T(128)} %bitcast.core, bf16[16,136,128]{2,1,0:T(8,128)(2,1)S(1)} %all-to-all-done.2.prefix, f32[128,512]{1,0:T(8,128)S(1)} %get-tuple-element.18.num, f32[8,512]{1,0:T(8,128)S(1)} %get-tuple-element.19.den, ...), custom_call_target="tpu_custom_call" | custom-call | flops 276824064 | bytes 2500000 | tf_op jit(solution)/shard_map/pallas_call | solution.py:280
  79.2 7.0 %collective-permute-start.5 = (bf16[4,136,512]{2,1,0:T(8,128)(2,1)S(1)}, bf16[4,136,512]{2,1,0:T(8,128)(2,1)S(1)}, u32[]{:S(2)}, u32[]{:S(2)}) collective-permute-start(bf16[4,136,512]{2,1,0:T(8,128)(2,1)S(1)} %get-tuple-element.22), channel_id=1, source_target_pairs={{0,1},{1,0},{2,3},{3,2},{4,5},{5,4},{6,7},{7,6},{8,9},{9,8},{10,11... | collective-permute-start | bytes 1671176 | tf_op jit(solution)/shard_map/ppermute | solution.py:289
  86.2 1.6 %collective-permute-done.5.received = bf16[4,136,512]{2,1,0:T(8,128)(2,1)S(1)} collective-permute-done((bf16[4,136,512]{2,1,0:T(8,128)(2,1)S(1)}, bf16[4,136,512]{2,1,0:T(8,128)(2,1)S(1)}, u32[]{:S(2)}, u32[]{:S(2)}) %collective-permute-start.5) | collective-permute-done | bytes 557088 | tf_op jit(solution)/shard_map/ppermute | solution.py:289
  87.8 0.2 shard_map.60
  88.0 0.0 copy-start
  88.0 12.0 %all_to_all.22.parts = bf16[4,136,512]{2,1,0:T(8,128)(2,1)S(1)} all-to-all(bf16[4,136,512]{2,1,0:T(8,128)(2,1)S(1)} %shard_map.60), channel_id=1, replica_groups={{0,2,4,6},{1,3,5,7},{8,10,12,14},{9,11,13,15},{16,18,20,22},{17,19,21,2..., dimensions={0} | all-to-all | bytes 1114112 | tf_op jit(solution)/shard_map/all_to_all | solution.py:221
  99.9 0.0 copy-done
  99.9 0.8 shard_map.61
  (2 shorter events, 0.0 us)
Async XLA Ops:
  0.0 21.9 %copy-start.1 = (bf16[1,1024,3,128]{3,1,2,0:T(8,128)(2,1)S(1)}, bf16[1,1024,3,128]{3,1,2,0:T(8,128)(2,1)}, u32[]{:S(2)}) copy-start(bf16[1,1024,3,128]{3,1,2,0:T(8,128)(2,1)} %param.6) | copy-start | bytes 2359300
  12.6 7.8 %copy-start.4 = (bf16[1,1024]{1,0:T(2,128)(2,1)S(1)}, bf16[1,1024]{1,0:T(2,128)(2,1)}, u32[]{:S(2)}) copy-start(bf16[1,1024]{1,0:T(2,128)(2,1)} %param.8) | copy-start | bytes 6148
  12.6 9.3 %collective-permute-start = (bf16[4,512,128]{2,1,0:T(8,128)(2,1)S(1)}, bf16[4,512,128]{2,1,0:T(8,128)(2,1)S(1)}, u32[]{:S(2)}, u32[]{:S(2)}) collective-permute-start(bf16[4,512,128]{2,1,0:T(8,128)(2,1)S(1)} %all_to_all.20.own), channel_id=1, source_target_pairs={{0,1},{1,0},{2,3},{3,2},{4,5},{5,4},{6,7},{7,6},{8,9},{9,8},{10,11... | collective-permute-start | bytes 1572872 | tf_op jit(solution)/shard_map/ppermute | solution.py:237
  46.8 12.4 %collective-permute-start.1 = (bf16[136,128]{1,0:T(8,128)(2,1)S(1)}, bf16[136,128]{1,0:T(8,128)(2,1)S(1)}, u32[]{:S(2)}, u32[]{:S(2)}) collective-permute-start(bf16[136,128]{1,0:T(8,128)(2,1)S(1)} %shard_map.56), channel_id=1, source_target_pairs={{0,128},{8,136},{16,144},{24,152},{32,160},{40,168},{48,176},{56,1... | collective-permute-start | bytes 104456 | tf_op jit(solution)/shard_map/ppermute | solution.py:225
  55.6 4.2 %collective-permute-start.3 = (bf16[136,128]{1,0:T(8,128)(2,1)S(1)}, bf16[136,128]{1,0:T(8,128)(2,1)S(1)}, u32[]{:S(2)}, u32[]{:S(2)}) collective-permute-start(bf16[136,128]{1,0:T(8,128)(2,1)S(1)} %shard_map.56), channel_id=1, source_target_pairs={{128,384},{136,392},{144,400},{152,408},{160,416},{168,424},{176,4... | collective-permute-start | bytes 104456 | tf_op jit(solution)/shard_map/ppermute | solution.py:225
  56.3 3.9 %collective-permute-start.2 = (bf16[136,128]{1,0:T(8,128)(2,1)S(1)}, bf16[136,128]{1,0:T(8,128)(2,1)S(1)}, u32[]{:S(2)}, u32[]{:S(2)}) collective-permute-start(bf16[136,128]{1,0:T(8,128)(2,1)S(1)} %shard_map.56), channel_id=1, source_target_pairs={{0,384},{8,392},{16,400},{24,408},{32,416},{40,424},{48,432},{56,4... | collective-permute-start | bytes 104456 | tf_op jit(solution)/shard_map/ppermute | solution.py:225
  59.2 1.0 collective-permute-start.4
  61.1 4.3 %copy-start.3 = (bf16[1,128,1024]{2,1,0:T(8,128)(2,1)S(1)}, bf16[1,128,1024]{2,1,0:T(8,128)(2,1)}, u32[]{:S(2)}) copy-start(bf16[1,128,1024]{2,1,0:T(8,128)(2,1)} %param.7) | copy-start | bytes 786436
  61.1 16.3 %all-to-all-start.2 = ((bf16[16,136,128]{2,1,0:T(8,128)(2,1)}), bf16[16,136,128]{2,1,0:T(8,128)(2,1)S(1)}, u32[]{:S(2)}, u32[]{:S(2)}) async-start(bf16[16,136,128]{2,1,0:T(8,128)(2,1)} %shard_map.57), calls=%async_computation.2 | async-start | bytes 1114112 | tf_op jit(solution)/shard_map/all_to_all | solution.py:221
  65.6 0.7 copy-start.2
  79.2 8.6 %collective-permute-start.5 = (bf16[4,136,512]{2,1,0:T(8,128)(2,1)S(1)}, bf16[4,136,512]{2,1,0:T(8,128)(2,1)S(1)}, u32[]{:S(2)}, u32[]{:S(2)}) collective-permute-start(bf16[4,136,512]{2,1,0:T(8,128)(2,1)S(1)} %get-tuple-element.22), channel_id=1, source_target_pairs={{0,1},{1,0},{2,3},{3,2},{4,5},{5,4},{6,7},{7,6},{8,9},{9,8},{10,11... | collective-permute-start | bytes 1671176 | tf_op jit(solution)/shard_map/ppermute | solution.py:289
  88.0 12.0 %copy-start = (bf16[512,128]{1,0:T(8,128)(2,1)S(1)}, bf16[512,128]{1,0:T(8,128)(2,1)}, u32[]{:S(2)}) copy-start(bf16[512,128]{1,0:T(8,128)(2,1)} %hidden.1) | copy-start | bytes 393220

commit v4 on v3

--- a/solution.py
+++ b/solution.py
@@ -11,8 +11,9 @@
 T = 512
 EPSILON = 1e-06
 SHIFTS = 32
-PLANE = 16
-PLANES = 4
+PLANE = 8
+PLANES = 8
+WIDE = 2 * PLANE
 MAIN = 2048 // PLANE
 EDGE = DH // PLANE
 SLICE = MAIN + 2 * EDGE
@@ -22,7 +23,7 @@
 SMEM = pl.BlockSpec(memory_space=pltpu.SMEM)
 X_GROUPS = [[0, 2, 4, 6], [1, 3, 5, 7]]
 NEAR_GROUPS = [[PLANE * z + y for y in range(PLANE)] for z in range(PLANES)]
-FAR_GROUPS = [[PLANE * z + y for z in range(PLANES)] for y in range(PLANE)]
+PAIR_SWAP = [(b, b ^ PLANE) for b in range(PLANE * PLANES)]
 CORE_SWAP = [(h, h ^ 1) for h in range(8)]
 
 
@@ -89,27 +90,19 @@
         k_t[:, rows] = turned[128:256]
         v_t[:, rows] = turned[256:384].astype(BF16)
     right = v_diag[...]
-    last = None
     for (shift, first), (_, second) in zip(feature_rows(k_t[0:DH, :]), feature_rows(k_t[DH:, :])):
         state = dot(jnp.concatenate([first, second], axis=1), right).astype(BF16)
         if shift == SHIFTS:
-            last = state
+            for y in range(PLANE):
+                sent[y, MAIN : MAIN + EDGE, :] = state[EDGE * y : EDGE * (y + 1)]
         else:
             y, start = divmod(DH * shift, MAIN)
             sent[y, start : start + DH, :] = state
     gram = dot(k_t[...].astype(BF16), k_nat[...])
     lane = lax.broadcasted_iota(jnp.int32, (DH, 128), 1)
     gram = jnp.where(lane < DH, gram[0:DH], gram[DH:]).astype(BF16)
-    edge = dot(edge_rows(128, DH, 0), last) + dot(edge_rows(128, DH, EDGE), gram)
-    sent[:, MAIN:, :] = edge.astype(BF16).reshape(PLANE, 2 * EDGE, 128)
-
-
-def edge_rows(rows, columns, offset):
-    row = lax.broadcasted_iota(jnp.int32, (rows, columns), 0)
-    column = lax.broadcasted_iota(jnp.int32, (rows, columns), 1)
-    place, a = (row, column) if rows == 128 else (column, row)
-    hit = place == 2 * EDGE * (a // EDGE) + a % EDGE + offset
-    return jnp.where(hit, 1.0, 0.0).astype(BF16)
+    for y in range(PLANE):
+        sent[y, MAIN + EDGE :, :] = gram[EDGE * y : EDGE * (y + 1)]
 
 
 def merge_kernel(blocks, total):
@@ -119,10 +112,11 @@
     total[...] = parts[0].astype(BF16)
 
 
-def spread_kernel(first, second, third, fourth, blocks, out):
+def spread_kernel(odd, partner, first, second, third, fourth, blocks, out):
     running = (first[...].astype(F32) + second[...].astype(F32)) + (
         third[...].astype(F32) + fourth[...].astype(F32)
     )
+    running += jnp.where(odd[0] == 1, partner[...].astype(F32), 0.0)
     for y in range(PLANE):
         out[y] = running.astype(BF16)
         if y < PLANE - 1:
@@ -156,8 +150,8 @@
 
 def finish_kernel(core, prefix, num, den, q_t, gain, weights, keep, give, feats):
     c = core[0]
-    edge = prefix[:, MAIN:, :].reshape(128, 128)
-    gram = dot(edge_rows(DH, 128, EDGE), edge).T.astype(BF16)
+    gram = jnp.concatenate([prefix[y, MAIN + EDGE :, :] for y in range(PLANE)], axis=0).astype(F32).T
+    gram = gram.astype(BF16)
     dens = []
     for h in range(2):
         queries = q_t[DH * h : DH * (h + 1), :]
@@ -170,9 +164,10 @@
     sums = [num[0:DH, :], num[DH:, :]]
     for group in range(9):
         if group < 8:
-            state = jnp.concatenate([prefix[2 * group, 0:MAIN, :], prefix[2 * group + 1, 0:MAIN, :]], axis=0)
+            y, start = divmod(256 * group, MAIN)
+            state = prefix[y, start : start + 256, :]
         else:
-            state = dot(edge_rows(DH, 128, 0), edge)
+            state = jnp.concatenate([prefix[y, MAIN : MAIN + EDGE, :] for y in range(PLANE)], axis=0)
         turned = state.astype(F32).T.astype(BF16)
         rows = pl.ds(256 * group, 256 if group < 8 else DH)
         for h in range(2):
@@ -223,7 +218,7 @@
 
 def forward(total, pairs):
     return lax.ppermute(
-        total, "seq", [(PLANE * a + i, PLANE * b + i) for a, b in pairs for i in range(PLANE)]
+        total, "seq", [(WIDE * a + i, WIDE * b + i) for a, b in pairs for i in range(WIDE)]
     )
 
 
@@ -265,16 +260,19 @@
         in_specs=[VMEM],
         out_specs=VMEM,
     )(blocks)
+    partner = lax.ppermute(total, "seq", PAIR_SWAP)
+    total = total + partner
     direct = forward(total, ((0, 1), (2, 3)))
-    earlier = [direct, forward(total, ((0, 3),)), forward(total, ((1, 3),))]
+    earlier = [direct, forward(total, ((1, 3),)), forward(total, ((0, 3),))]
     earlier.append(forward(total + direct, ((1, 2),)))
+    odd = ((lax.axis_index("seq") // PLANE) & 1).astype(jnp.int32)[None]
     spread = call(
         spread_kernel,
         shape((PLANE, SLICE, 128), BF16),
         moved=1300000,
-        in_specs=[VMEM] * 5,
+        in_specs=[SMEM] + [VMEM] * 6,
         out_specs=VMEM,
-    )(*earlier, blocks)
+    )(odd, partner, *earlier, blocks)
     spread = exchange(spread, "seq", NEAR_GROUPS)
     partial = shape((4, 136, T), BF16)
     keep, give = call(

time: 101 us -> 98.9 us (0.979)
  the two profiles are of different devices: /device:TPU:1 before, /device:TPU:352 now
where the time goes in v4:
time: 98.9 us; the launch traced here: 98.4 us
  blocking collectives  41.7 us (42%)
  waiting for transfers between devices  29.1 us (29%)
  starting transfers between devices  19 us (19%)
  Pallas kernels  6.54 us (7%)
  local copies, waits for them, and re-layouts  1.88 us (2%)
    all_to_all x3, blocking collectives, exchange(): return lax.all_to_all(blocks, axis, 0, 0, axis_index_groups=groups)  41.7 us
    ppermute x4, waiting for transfers between devices, forward(): lax.ppermute(total, 'seq', [(WIDE * a + i, WIDE * b + i) for a, b in pair...  14.1 us
    all_to_all x1, waiting for transfers between devices, exchange(): return lax.all_to_all(blocks, axis, 0, 0, axis_index_groups=groups)  7.51 us
    ppermute x4, starting transfers between devices, forward(): lax.ppermute(total, 'seq', [(WIDE * a + i, WIDE * b + i) for a, b in pair...  6.92 us
    all_to_all x1, starting transfers between devices, exchange(): return lax.all_to_all(blocks, axis, 0, 0, axis_index_groups=groups)  4.79 us
    ppermute x1, waiting for transfers between devices, shards(): partner = lax.ppermute(total, 'seq', PAIR_SWAP)  3.73 us
    ppermute x1, starting transfers between devices, shards(): partner = lax.ppermute(total, 'seq', PAIR_SWAP)  3.36 us
    pallas_call x1, Pallas kernels, shards(): call(project_kernel, (shape((PLANE, SLICE, 128), BF16), shape((128, T), B...  2.25 us
  transfers between devices with their start and end apart: 8, of which 6 were waited for; matrix products, arithmetic and copies ran while one was open for 0% of the time, Pallas kernels for 1%

profile of v4, /device:TPU:352, one launch (start us, length us, event | category | flops | bytes accessed | tf_op | source)
XLA Modules:
  0.0 98.4 jit_solution(7449098006728833104)
XLA Ops:
  0.0 0.0 copy-start.1
  0.0 1.0 %broadcast_in_dim.11 = bf16[4,512,128]{2,1,0:T(8,128)(2,1)S(1)} broadcast(bf16[512,128]{1,0:T(8,128)(2,1)} %hidden.1), dimensions={1,2} | broadcast | bytes 655360 | tf_op jit(solution)/shard_map/broadcast_in_dim | solution.py:231
  1.1 13.6 %all_to_all.20.own = bf16[4,512,128]{2,1,0:T(8,128)(2,1)S(1)} all-to-all(bf16[4,512,128]{2,1,0:T(8,128)(2,1)S(1)} %broadcast_in_dim.11), channel_id=1, replica_groups={{0,2,4,6},{1,3,5,7},{8,10,12,14},{9,11,13,15},{16,18,20,22},{17,19,21,2..., dimensions={0} | all-to-all | bytes 1048576 | tf_op jit(solution)/shard_map/all_to_all | solution.py:216
  14.6 0.0 copy-start.4
  14.6 2.0 %collective-permute-start = (bf16[4,512,128]{2,1,0:T(8,128)(2,1)S(1)}, bf16[4,512,128]{2,1,0:T(8,128)(2,1)S(1)}, u32[]{:S(2)}, u32[]{:S(2)}) collective-permute-start(bf16[4,512,128]{2,1,0:T(8,128)(2,1)S(1)} %all_to_all.20.own), channel_id=1, source_target_pairs={{0,1},{1,0},{2,3},{3,2},{4,5},{5,4},{6,7},{7,6},{8,9},{9,8},{10,11... | collective-permute-start | bytes 1572872 | tf_op jit(solution)/shard_map/ppermute | solution.py:232
  16.7 0.0 copy-done.4
  16.7 1.8 %collective-permute-done.other = bf16[4,512,128]{2,1,0:T(8,128)(2,1)S(1)} collective-permute-done((bf16[4,512,128]{2,1,0:T(8,128)(2,1)S(1)}, bf16[4,512,128]{2,1,0:T(8,128)(2,1)S(1)}, u32[]{:S(2)}, u32[]{:S(2)}) %collective-permute-start) | collective-permute-done | bytes 524320 | tf_op jit(solution)/shard_map/ppermute | solution.py:232
  18.5 0.0 copy-done.1
  18.6 2.3 %shard_map.55 = (bf16[8,272,128]{2,1,0:T(8,128)(2,1)S(1)}, bf16[128,512]{1,0:T(8,128)(2,1)S(1)}, bf16[512,128]{1,0:T(8,128)(2,1)S(1)}, bf16[128,512]{1,0:T(8,128)(2,1)S(1)}) custom-call(s32[1]{0:T(128)} %bitcast.core, bf16[4,512,128]{2,1,0:T(8,128)(2,1)S(1)} %all_to_all.20.own, bf16[4,512,128]{2,1,0:T(8,128)(2,1)S(1)} %collective-permute-done.other, ...), custom_call_target="tpu_custom_call" | custom-call | flops 956301312 | bytes 3000000 | tf_op jit(solution)/shard_map/pallas_call | solution.py:233
  20.8 15.2 %all_to_all.21.blocks = bf16[8,272,128]{2,1,0:T(8,128)(2,1)S(1)} all-to-all(bf16[8,272,128]{2,1,0:T(8,128)(2,1)S(1)} %get-tuple-element.14), channel_id=1, replica_groups={{0,8,16,24,32,40,48,56},{64,72,80,88,96,104,112,120},{128,136,144,152,1..., dimensions={0} | all-to-all | bytes 1114112 | tf_op jit(solution)/shard_map/all_to_all | solution.py:216
  36.0 0.1 shard_map.56
  36.1 3.4 %collective-permute-start.1 = (bf16[272,128]{1,0:T(8,128)(2,1)S(1)}, bf16[272,128]{1,0:T(8,128)(2,1)S(1)}, u32[]{:S(2)}, u32[]{:S(2)}) collective-permute-start(bf16[272,128]{1,0:T(8,128)(2,1)S(1)} %shard_map.56), channel_id=1, source_target_pairs={{0,64},{8,72},{16,80},{24,88},{32,96},{40,104},{48,112},{56,120},{... | collective-permute-start | bytes 208904 | tf_op jit(solution)/shard_map/ppermute | solution.py:263
  39.5 3.7 %collective-permute-done.1.partner = bf16[272,128]{1,0:T(8,128)(2,1)S(1)} collective-permute-done((bf16[272,128]{1,0:T(8,128)(2,1)S(1)}, bf16[272,128]{1,0:T(8,128)(2,1)S(1)}, u32[]{:S(2)}, u32[]{:S(2)}) %collective-permute-start.1) | collective-permute-done | bytes 69664 | tf_op jit(solution)/shard_map/ppermute | solution.py:263
  43.2 4.3 %collective-permute-start.2 = (bf16[272,128]{1,0:T(8,128)(2,1)S(1)}, bf16[272,128]{1,0:T(8,128)(2,1)S(1)}, u32[]{:S(2)}, u32[]{:S(2)}) collective-permute-start(bf16[272,128]{1,0:T(8,128)(2,1)S(1)} %add.7), channel_id=1, source_target_pairs={{0,128},{8,136},{16,144},{24,152},{32,160},{40,168},{48,176},{56,1... | collective-permute-start | bytes 208904 | tf_op jit(solution)/shard_map/ppermute | solution.py:220
  47.5 0.7 collective-permute-start.4
  48.2 0.7 collective-permute-start.3
  48.9 0.6 collective-permute-done.2.first
  49.5 1.3 %collective-permute-start.5 = (bf16[272,128]{1,0:T(8,128)(2,1)S(1)}, bf16[272,128]{1,0:T(8,128)(2,1)S(1)}, u32[]{:S(2)}, u32[]{:S(2)}) collective-permute-start(bf16[272,128]{1,0:T(8,128)(2,1)S(1)} %add.8), channel_id=1, source_target_pairs={{128,256},{136,264},{144,272},{152,280},{160,288},{168,296},{176,3... | collective-permute-start | bytes 208904 | tf_op jit(solution)/shard_map/ppermute | solution.py:220
  50.8 0.0 collective-permute-done.4.third
  50.8 0.0 collective-permute-done.3.second
  50.8 13.5 %collective-permute-done.5.fourth = bf16[272,128]{1,0:T(8,128)(2,1)S(1)} collective-permute-done((bf16[272,128]{1,0:T(8,128)(2,1)S(1)}, bf16[272,128]{1,0:T(8,128)(2,1)S(1)}, u32[]{:S(2)}, u32[]{:S(2)}) %collective-permute-start.5) | collective-permute-done | bytes 69664 | tf_op jit(solution)/shard_map/ppermute | solution.py:220
  64.3 0.9 shard_map.57
  65.2 0.0 copy-start.3
  65.2 4.8 %all-to-all-start.2 = ((bf16[8,272,128]{2,1,0:T(8,128)(2,1)}), bf16[8,272,128]{2,1,0:T(8,128)(2,1)S(1)}, u32[]{:S(2)}, u32[]{:S(2)}) async-start(bf16[8,272,128]{2,1,0:T(8,128)(2,1)} %shard_map.57), calls=%async_computation.2 | async-start | bytes 1114112 | tf_op jit(solution)/shard_map/all_to_all | solution.py:216
  70.0 0.0 copy-done.3
  70.0 0.2 copy.6
  70.2 0.0 copy-start.2
  70.2 0.6 copy-done.2
  70.9 0.8 shard_map.58
  71.7 7.5 %all-to-all-done.2.prefix = bf16[8,272,128]{2,1,0:T(8,128)(2,1)S(1)} async-done(((bf16[8,272,128]{2,1,0:T(8,128)(2,1)}), bf16[8,272,128]{2,1,0:T(8,128)(2,1)S(1)}, u32[]{:S(2)}, u32[]{:S(2)}) %all-to-all-start.2) | async-done | bytes 557088 | tf_op jit(solution)/shard_map/all_to_all | solution.py:216
  79.2 1.5 %shard_map.59 = (bf16[4,136,512]{2,1,0:T(8,128)(2,1)S(1)}, bf16[4,136,512]{2,1,0:T(8,128)(2,1)S(1)}) custom-call(s32[1]{0:T(128)} %bitcast.core, bf16[8,272,128]{2,1,0:T(8,128)(2,1)S(1)} %all-to-all-done.2.prefix, f32[128,512]{1,0:T(8,128)S(1)} %get-tuple-element.18.num, f32[8,512]{1,0:T(8,128)S(1)} %get-tuple-element.19.den, ...), custom_call_target="tpu_custom_call" | custom-call | flops 276824064 | bytes 2500000 | tf_op jit(solution)/shard_map/pallas_call | solution.py:278
  80.7 1.9 %collective-permute-start.6 = (bf16[4,136,512]{2,1,0:T(8,128)(2,1)S(1)}, bf16[4,136,512]{2,1,0:T(8,128)(2,1)S(1)}, u32[]{:S(2)}, u32[]{:S(2)}) collective-permute-start(bf16[4,136,512]{2,1,0:T(8,128)(2,1)S(1)} %get-tuple-element.22), channel_id=1, source_target_pairs={{0,1},{1,0},{2,3},{3,2},{4,5},{5,4},{6,7},{7,6},{8,9},{9,8},{10,11... | collective-permute-start | bytes 1671176 | tf_op jit(solution)/shard_map/ppermute | solution.py:287
  82.6 1.9 %collective-permute-done.6.received = bf16[4,136,512]{2,1,0:T(8,128)(2,1)S(1)} collective-permute-done((bf16[4,136,512]{2,1,0:T(8,128)(2,1)S(1)}, bf16[4,136,512]{2,1,0:T(8,128)(2,1)S(1)}, u32[]{:S(2)}, u32[]{:S(2)}) %collective-permute-start.6) | collective-permute-done | bytes 557088 | tf_op jit(solution)/shard_map/ppermute | solution.py:287
  84.5 0.2 shard_map.60
  84.7 0.0 copy-start
  84.7 12.9 %all_to_all.22.parts = bf16[4,136,512]{2,1,0:T(8,128)(2,1)S(1)} all-to-all(bf16[4,136,512]{2,1,0:T(8,128)(2,1)S(1)} %shard_map.60), channel_id=1, replica_groups={{0,2,4,6},{1,3,5,7},{8,10,12,14},{9,11,13,15},{16,18,20,22},{17,19,21,2..., dimensions={0} | all-to-all | bytes 1114112 | tf_op jit(solution)/shard_map/all_to_all | solution.py:216
  97.6 0.0 copy-done
  97.6 0.8 shard_map.61
  (3 shorter events, 0.0 us)
Async XLA Ops:
  0.0 18.6 %copy-start.1 = (bf16[1,1024,3,128]{3,1,2,0:T(8,128)(2,1)S(1)}, bf16[1,1024,3,128]{3,1,2,0:T(8,128)(2,1)}, u32[]{:S(2)}) copy-start(bf16[1,1024,3,128]{3,1,2,0:T(8,128)(2,1)} %param.6) | copy-start | bytes 2359300
  14.6 2.1 %copy-start.4 = (bf16[1,1024]{1,0:T(2,128)(2,1)S(1)}, bf16[1,1024]{1,0:T(2,128)(2,1)}, u32[]{:S(2)}) copy-start(bf16[1,1024]{1,0:T(2,128)(2,1)} %param.8) | copy-start | bytes 6148
  14.6 3.9 %collective-permute-start = (bf16[4,512,128]{2,1,0:T(8,128)(2,1)S(1)}, bf16[4,512,128]{2,1,0:T(8,128)(2,1)S(1)}, u32[]{:S(2)}, u32[]{:S(2)}) collective-permute-start(bf16[4,512,128]{2,1,0:T(8,128)(2,1)S(1)} %all_to_all.20.own), channel_id=1, source_target_pairs={{0,1},{1,0},{2,3},{3,2},{4,5},{5,4},{6,7},{7,6},{8,9},{9,8},{10,11... | collective-permute-start | bytes 1572872 | tf_op jit(solution)/shard_map/ppermute | solution.py:232
  36.1 7.1 %collective-permute-start.1 = (bf16[272,128]{1,0:T(8,128)(2,1)S(1)}, bf16[272,128]{1,0:T(8,128)(2,1)S(1)}, u32[]{:S(2)}, u32[]{:S(2)}) collective-permute-start(bf16[272,128]{1,0:T(8,128)(2,1)S(1)} %shard_map.56), channel_id=1, source_target_pairs={{0,64},{8,72},{16,80},{24,88},{32,96},{40,104},{48,112},{56,120},{... | collective-permute-start | bytes 208904 | tf_op jit(solution)/shard_map/ppermute | solution.py:263
  43.2 6.2 %collective-permute-start.2 = (bf16[272,128]{1,0:T(8,128)(2,1)S(1)}, bf16[272,128]{1,0:T(8,128)(2,1)S(1)}, u32[]{:S(2)}, u32[]{:S(2)}) collective-permute-start(bf16[272,128]{1,0:T(8,128)(2,1)S(1)} %add.7), channel_id=1, source_target_pairs={{0,128},{8,136},{16,144},{24,152},{32,160},{40,168},{48,176},{56,1... | collective-permute-start | bytes 208904 | tf_op jit(solution)/shard_map/ppermute | solution.py:220
  47.5 3.3 %collective-permute-start.4 = (bf16[272,128]{1,0:T(8,128)(2,1)S(1)}, bf16[272,128]{1,0:T(8,128)(2,1)S(1)}, u32[]{:S(2)}, u32[]{:S(2)}) collective-permute-start(bf16[272,128]{1,0:T(8,128)(2,1)S(1)} %add.7), channel_id=1, source_target_pairs={{0,384},{8,392},{16,400},{24,408},{32,416},{40,424},{48,432},{56,4... | collective-permute-start | bytes 208904 | tf_op jit(solution)/shard_map/ppermute | solution.py:220
  48.2 2.6 %collective-permute-start.3 = (bf16[272,128]{1,0:T(8,128)(2,1)S(1)}, bf16[272,128]{1,0:T(8,128)(2,1)S(1)}, u32[]{:S(2)}, u32[]{:S(2)}) collective-permute-start(bf16[272,128]{1,0:T(8,128)(2,1)S(1)} %add.7), channel_id=1, source_target_pairs={{128,384},{136,392},{144,400},{152,408},{160,416},{168,424},{176,4... | collective-permute-start | bytes 208904 | tf_op jit(solution)/shard_map/ppermute | solution.py:220
  49.5 14.8 %collective-permute-start.5 = (bf16[272,128]{1,0:T(8,128)(2,1)S(1)}, bf16[272,128]{1,0:T(8,128)(2,1)S(1)}, u32[]{:S(2)}, u32[]{:S(2)}) collective-permute-start(bf16[272,128]{1,0:T(8,128)(2,1)S(1)} %add.8), channel_id=1, source_target_pairs={{128,256},{136,264},{144,272},{152,280},{160,288},{168,296},{176,3... | collective-permute-start | bytes 208904 | tf_op jit(solution)/shard_map/ppermute | solution.py:220
  65.2 4.8 %copy-start.3 = (bf16[1,128,1024]{2,1,0:T(8,128)(2,1)S(1)}, bf16[1,128,1024]{2,1,0:T(8,128)(2,1)}, u32[]{:S(2)}) copy-start(bf16[1,128,1024]{2,1,0:T(8,128)(2,1)} %param.7) | copy-start | bytes 786436
  65.2 13.9 %all-to-all-start.2 = ((bf16[8,272,128]{2,1,0:T(8,128)(2,1)}), bf16[8,272,128]{2,1,0:T(8,128)(2,1)S(1)}, u32[]{:S(2)}, u32[]{:S(2)}) async-start(bf16[8,272,128]{2,1,0:T(8,128)(2,1)} %shard_map.57), calls=%async_computation.2 | async-start | bytes 1114112 | tf_op jit(solution)/shard_map/all_to_all | solution.py:216
  70.2 0.7 copy-start.2
  80.7 3.9 %collective-permute-start.6 = (bf16[4,136,512]{2,1,0:T(8,128)(2,1)S(1)}, bf16[4,136,512]{2,1,0:T(8,128)(2,1)S(1)}, u32[]{:S(2)}, u32[]{:S(2)}) collective-permute-start(bf16[4,136,512]{2,1,0:T(8,128)(2,1)S(1)} %get-tuple-element.22), channel_id=1, source_target_pairs={{0,1},{1,0},{2,3},{3,2},{4,5},{5,4},{6,7},{7,6},{8,9},{9,8},{10,11... | collective-permute-start | bytes 1671176 | tf_op jit(solution)/shard_map/ppermute | solution.py:287
  84.7 12.9 %copy-start = (bf16[512,128]{1,0:T(8,128)(2,1)S(1)}, bf16[512,128]{1,0:T(8,128)(2,1)}, u32[]{:S(2)}) copy-start(bf16[512,128]{1,0:T(8,128)(2,1)} %hidden.1) | copy-start | bytes 393220

commit v5 on v4

--- a/solution.py
+++ b/solution.py
@@ -112,10 +112,9 @@
     total[...] = parts[0].astype(BF16)
 
 
-def spread_kernel(odd, partner, first, second, third, fourth, blocks, out):
-    running = (first[...].astype(F32) + second[...].astype(F32)) + (
-        third[...].astype(F32) + fourth[...].astype(F32)
-    )
+def spread_kernel(odd, group, partner, swapped, second, third, blocks, out):
+    running = second[...].astype(F32) + third[...].astype(F32)
+    running += jnp.where(group[0] > 0, swapped[...].astype(F32), 0.0)
     running += jnp.where(odd[0] == 1, partner[...].astype(F32), 0.0)
     for y in range(PLANE):
         out[y] = running.astype(BF16)
@@ -262,17 +261,18 @@
     )(blocks)
     partner = lax.ppermute(total, "seq", PAIR_SWAP)
     total = total + partner
-    direct = forward(total, ((0, 1), (2, 3)))
-    earlier = [direct, forward(total, ((1, 3),)), forward(total, ((0, 3),))]
-    earlier.append(forward(total + direct, ((1, 2),)))
-    odd = ((lax.axis_index("seq") // PLANE) & 1).astype(jnp.int32)[None]
+    swapped = forward(total, ((0, 1), (1, 0)))
+    earlier = [swapped, forward(total, ((2, 3),)), forward(total + swapped, ((1, 2), (0, 3)))]
+    place = lax.axis_index("seq")
+    odd = ((place // PLANE) & 1).astype(jnp.int32)[None]
+    group = (place // WIDE).astype(jnp.int32)[None]
     spread = call(
         spread_kernel,
         shape((PLANE, SLICE, 128), BF16),
         moved=1300000,
-        in_specs=[SMEM] + [VMEM] * 6,
+        in_specs=[SMEM] * 2 + [VMEM] * 5,
         out_specs=VMEM,
-    )(odd, partner, *earlier, blocks)
+    )(odd, group, partner, *earlier, blocks)
     spread = exchange(spread, "seq", NEAR_GROUPS)
     partial = shape((4, 136, T), BF16)
     keep, give = call(

time: 98.9 us -> 96.7 us (0.978)
  the two profiles are of different devices: /device:TPU:352 before, /device:TPU:1 now
where the time goes in v5:
time: 96.7 us; the launch traced here: 96.2 us
  blocking collectives  36.6 us (38%)
  starting transfers between devices  35.6 us (37%)
  waiting for transfers between devices  15.4 us (16%)
  Pallas kernels  6.52 us (7%)
  local copies, waits for them, and re-layouts  1.88 us (2%)
    all_to_all x3, blocking collectives, exchange(): return lax.all_to_all(blocks, axis, 0, 0, axis_index_groups=groups)  36.6 us
    ppermute x3, starting transfers between devices, forward(): lax.ppermute(total, 'seq', [(WIDE * a + i, WIDE * b + i) for a, b in pair...  11.8 us
    ppermute x1, starting transfers between devices, shards(): other = lax.ppermute(own, 'head', CORE_SWAP)  7.78 us
    ppermute x1, starting transfers between devices, shards(): received = lax.ppermute(give, 'head', CORE_SWAP)  7.42 us
    all_to_all x1, waiting for transfers between devices, exchange(): return lax.all_to_all(blocks, axis, 0, 0, axis_index_groups=groups)  5.53 us
    ppermute x1, starting transfers between devices, shards(): partner = lax.ppermute(total, 'seq', PAIR_SWAP)  4.9 us
    ppermute x3, waiting for transfers between devices, forward(): lax.ppermute(total, 'seq', [(WIDE * a + i, WIDE * b + i) for a, b in pair...  4.4 us
    all_to_all x1, starting transfers between devices, exchange(): return lax.all_to_all(blocks, axis, 0, 0, axis_index_groups=groups)  3.67 us
  transfers between devices with their start and end apart: 7, of which 6 were waited for; matrix products, arithmetic and copies ran while one was open for 0% of the time, Pallas kernels for 1%

profile of v5, /device:TPU:1, one launch (start us, length us, event | category | flops | bytes accessed | tf_op | source)
XLA Modules:
  0.0 96.2 jit_solution(12896087753690385108)
XLA Ops:
  0.0 0.0 copy-start.1
  0.0 1.0 %broadcast_in_dim.15 = bf16[4,512,128]{2,1,0:T(8,128)(2,1)S(1)} broadcast(bf16[512,128]{1,0:T(8,128)(2,1)} %hidden.1), dimensions={1,2} | broadcast | bytes 655360 | tf_op jit(solution)/shard_map/broadcast_in_dim | solution.py:230
  1.1 11.6 %all_to_all.20.own = bf16[4,512,128]{2,1,0:T(8,128)(2,1)S(1)} all-to-all(bf16[4,512,128]{2,1,0:T(8,128)(2,1)S(1)} %broadcast_in_dim.15), channel_id=1, replica_groups={{0,2,4,6},{1,3,5,7},{8,10,12,14},{9,11,13,15},{16,18,20,22},{17,19,21,2..., dimensions={0} | all-to-all | bytes 1048576 | tf_op jit(solution)/shard_map/all_to_all | solution.py:215
  12.6 0.0 copy-start.4
  12.6 7.8 %collective-permute-start = (bf16[4,512,128]{2,1,0:T(8,128)(2,1)S(1)}, bf16[4,512,128]{2,1,0:T(8,128)(2,1)S(1)}, u32[]{:S(2)}, u32[]{:S(2)}) collective-permute-start(bf16[4,512,128]{2,1,0:T(8,128)(2,1)S(1)} %all_to_all.20.own), channel_id=1, source_target_pairs={{0,1},{1,0},{2,3},{3,2},{4,5},{5,4},{6,7},{7,6},{8,9},{9,8},{10,11... | collective-permute-start | bytes 1572872 | tf_op jit(solution)/shard_map/ppermute | solution.py:231
  20.4 0.0 copy-done.4
  20.4 1.5 %collective-permute-done.other = bf16[4,512,128]{2,1,0:T(8,128)(2,1)S(1)} collective-permute-done((bf16[4,512,128]{2,1,0:T(8,128)(2,1)S(1)}, bf16[4,512,128]{2,1,0:T(8,128)(2,1)S(1)}, u32[]{:S(2)}, u32[]{:S(2)}) %collective-permute-start) | collective-permute-done | bytes 524320 | tf_op jit(solution)/shard_map/ppermute | solution.py:231
  21.9 0.0 copy-done.1
  21.9 2.3 %shard_map.55 = (bf16[8,272,128]{2,1,0:T(8,128)(2,1)S(1)}, bf16[128,512]{1,0:T(8,128)(2,1)S(1)}, bf16[512,128]{1,0:T(8,128)(2,1)S(1)}, bf16[128,512]{1,0:T(8,128)(2,1)S(1)}) custom-call(s32[1]{0:T(128)} %bitcast.core, bf16[4,512,128]{2,1,0:T(8,128)(2,1)S(1)} %all_to_all.20.own, bf16[4,512,128]{2,1,0:T(8,128)(2,1)S(1)} %collective-permute-done.other, ...), custom_call_target="tpu_custom_call" | custom-call | flops 956301312 | bytes 3000000 | tf_op jit(solution)/shard_map/pallas_call | solution.py:232
  24.2 13.1 %all_to_all.21.blocks = bf16[8,272,128]{2,1,0:T(8,128)(2,1)S(1)} all-to-all(bf16[8,272,128]{2,1,0:T(8,128)(2,1)S(1)} %get-tuple-element.14), channel_id=1, replica_groups={{0,8,16,24,32,40,48,56},{64,72,80,88,96,104,112,120},{128,136,144,152,1..., dimensions={0} | all-to-all | bytes 1114112 | tf_op jit(solution)/shard_map/all_to_all | solution.py:215
  37.3 0.1 shard_map.56
  37.3 4.9 %collective-permute-start.1 = (bf16[272,128]{1,0:T(8,128)(2,1)S(1)}, bf16[272,128]{1,0:T(8,128)(2,1)S(1)}, u32[]{:S(2)}, u32[]{:S(2)}) collective-permute-start(bf16[272,128]{1,0:T(8,128)(2,1)S(1)} %shard_map.56), channel_id=1, source_target_pairs={{0,64},{8,72},{16,80},{24,88},{32,96},{40,104},{48,112},{56,120},{... | collective-permute-start | bytes 208904 | tf_op jit(solution)/shard_map/ppermute | solution.py:262
  42.2 2.4 %collective-permute-done.1.partner = bf16[272,128]{1,0:T(8,128)(2,1)S(1)} collective-permute-done((bf16[272,128]{1,0:T(8,128)(2,1)S(1)}, bf16[272,128]{1,0:T(8,128)(2,1)S(1)}, u32[]{:S(2)}, u32[]{:S(2)}) %collective-permute-start.1) | collective-permute-done | bytes 69664 | tf_op jit(solution)/shard_map/ppermute | solution.py:262
  44.7 8.8 %collective-permute-start.2 = (bf16[272,128]{1,0:T(8,128)(2,1)S(1)}, bf16[272,128]{1,0:T(8,128)(2,1)S(1)}, u32[]{:S(2)}, u32[]{:S(2)}) collective-permute-start(bf16[272,128]{1,0:T(8,128)(2,1)S(1)} %add.8), channel_id=1, source_target_pairs={{0,128},{8,136},{16,144},{24,152},{32,160},{40,168},{48,176},{56,1... | collective-permute-start | bytes 208904 | tf_op jit(solution)/shard_map/ppermute | solution.py:219
  53.5 0.7 collective-permute-start.3
  54.2 1.1 %collective-permute-done.2.swapped = bf16[272,128]{1,0:T(8,128)(2,1)S(1)} collective-permute-done((bf16[272,128]{1,0:T(8,128)(2,1)S(1)}, bf16[272,128]{1,0:T(8,128)(2,1)S(1)}, u32[]{:S(2)}, u32[]{:S(2)}) %collective-permute-start.2) | collective-permute-done | bytes 69664 | tf_op jit(solution)/shard_map/ppermute | solution.py:219
  55.3 2.3 %collective-permute-start.4 = (bf16[272,128]{1,0:T(8,128)(2,1)S(1)}, bf16[272,128]{1,0:T(8,128)(2,1)S(1)}, u32[]{:S(2)}, u32[]{:S(2)}) collective-permute-start(bf16[272,128]{1,0:T(8,128)(2,1)S(1)} %add.9), channel_id=1, source_target_pairs={{128,256},{136,264},{144,272},{152,280},{160,288},{168,296},{176,3... | collective-permute-start | bytes 208904 | tf_op jit(solution)/shard_map/ppermute | solution.py:219
  57.7 0.0 collective-permute-done.3.second
  57.7 3.3 %collective-permute-done.4.third = bf16[272,128]{1,0:T(8,128)(2,1)S(1)} collective-permute-done((bf16[272,128]{1,0:T(8,128)(2,1)S(1)}, bf16[272,128]{1,0:T(8,128)(2,1)S(1)}, u32[]{:S(2)}, u32[]{:S(2)}) %collective-permute-start.4) | collective-permute-done | bytes 69664 | tf_op jit(solution)/shard_map/ppermute | solution.py:219
  61.0 0.9 shard_map.57
  61.9 0.0 copy-start.3
  61.9 3.7 %all-to-all-start.2 = ((bf16[8,272,128]{2,1,0:T(8,128)(2,1)}), bf16[8,272,128]{2,1,0:T(8,128)(2,1)S(1)}, u32[]{:S(2)}, u32[]{:S(2)}) async-start(bf16[8,272,128]{2,1,0:T(8,128)(2,1)} %shard_map.57), calls=%async_computation.2 | async-start | bytes 1114112 | tf_op jit(solution)/shard_map/all_to_all | solution.py:215
  65.6 0.0 copy-done.3
  65.6 0.2 copy.6
  65.8 0.0 copy-start.2
  65.8 0.6 copy-done.2
  66.4 0.8 shard_map.58
  67.2 5.5 %all-to-all-done.2.prefix = bf16[8,272,128]{2,1,0:T(8,128)(2,1)S(1)} async-done(((bf16[8,272,128]{2,1,0:T(8,128)(2,1)}), bf16[8,272,128]{2,1,0:T(8,128)(2,1)S(1)}, u32[]{:S(2)}, u32[]{:S(2)}) %all-to-all-start.2) | async-done | bytes 557088 | tf_op jit(solution)/shard_map/all_to_all | solution.py:215
  72.8 1.5 %shard_map.59 = (bf16[4,136,512]{2,1,0:T(8,128)(2,1)S(1)}, bf16[4,136,512]{2,1,0:T(8,128)(2,1)S(1)}) custom-call(s32[1]{0:T(128)} %bitcast.core, bf16[8,272,128]{2,1,0:T(8,128)(2,1)S(1)} %all-to-all-done.2.prefix, f32[128,512]{1,0:T(8,128)S(1)} %get-tuple-element.18.num, f32[8,512]{1,0:T(8,128)S(1)} %get-tuple-element.19.den, ...), custom_call_target="tpu_custom_call" | custom-call | flops 276824064 | bytes 2500000 | tf_op jit(solution)/shard_map/pallas_call | solution.py:278
  74.3 7.4 %collective-permute-start.5 = (bf16[4,136,512]{2,1,0:T(8,128)(2,1)S(1)}, bf16[4,136,512]{2,1,0:T(8,128)(2,1)S(1)}, u32[]{:S(2)}, u32[]{:S(2)}) collective-permute-start(bf16[4,136,512]{2,1,0:T(8,128)(2,1)S(1)} %get-tuple-element.22), channel_id=1, source_target_pairs={{0,1},{1,0},{2,3},{3,2},{4,5},{5,4},{6,7},{7,6},{8,9},{9,8},{10,11... | collective-permute-start | bytes 1671176 | tf_op jit(solution)/shard_map/ppermute | solution.py:287
  81.7 1.6 %collective-permute-done.5.received = bf16[4,136,512]{2,1,0:T(8,128)(2,1)S(1)} collective-permute-done((bf16[4,136,512]{2,1,0:T(8,128)(2,1)S(1)}, bf16[4,136,512]{2,1,0:T(8,128)(2,1)S(1)}, u32[]{:S(2)}, u32[]{:S(2)}) %collective-permute-start.5) | collective-permute-done | bytes 557088 | tf_op jit(solution)/shard_map/ppermute | solution.py:287
  83.3 0.2 shard_map.60
  83.4 0.0 copy-start
  83.4 12.0 %all_to_all.22.parts = bf16[4,136,512]{2,1,0:T(8,128)(2,1)S(1)} all-to-all(bf16[4,136,512]{2,1,0:T(8,128)(2,1)S(1)} %shard_map.60), channel_id=1, replica_groups={{0,2,4,6},{1,3,5,7},{8,10,12,14},{9,11,13,15},{16,18,20,22},{17,19,21,2..., dimensions={0} | all-to-all | bytes 1114112 | tf_op jit(solution)/shard_map/all_to_all | solution.py:215
  95.4 0.0 copy-done
  95.4 0.8 shard_map.61
  (3 shorter events, 0.1 us)
Async XLA Ops:
  0.0 21.9 %copy-start.1 = (bf16[1,1024,3,128]{3,1,2,0:T(8,128)(2,1)S(1)}, bf16[1,1024,3,128]{3,1,2,0:T(8,128)(2,1)}, u32[]{:S(2)}) copy-start(bf16[1,1024,3,128]{3,1,2,0:T(8,128)(2,1)} %param.6) | copy-start | bytes 2359300
  12.6 7.8 %copy-start.4 = (bf16[1,1024]{1,0:T(2,128)(2,1)S(1)}, bf16[1,1024]{1,0:T(2,128)(2,1)}, u32[]{:S(2)}) copy-start(bf16[1,1024]{1,0:T(2,128)(2,1)} %param.8) | copy-start | bytes 6148
  12.6 9.3 %collective-permute-start = (bf16[4,512,128]{2,1,0:T(8,128)(2,1)S(1)}, bf16[4,512,128]{2,1,0:T(8,128)(2,1)S(1)}, u32[]{:S(2)}, u32[]{:S(2)}) collective-permute-start(bf16[4,512,128]{2,1,0:T(8,128)(2,1)S(1)} %all_to_all.20.own), channel_id=1, source_target_pairs={{0,1},{1,0},{2,3},{3,2},{4,5},{5,4},{6,7},{7,6},{8,9},{9,8},{10,11... | collective-permute-start | bytes 1572872 | tf_op jit(solution)/shard_map/ppermute | solution.py:231
  37.3 7.3 %collective-permute-start.1 = (bf16[272,128]{1,0:T(8,128)(2,1)S(1)}, bf16[272,128]{1,0:T(8,128)(2,1)S(1)}, u32[]{:S(2)}, u32[]{:S(2)}) collective-permute-start(bf16[272,128]{1,0:T(8,128)(2,1)S(1)} %shard_map.56), channel_id=1, source_target_pairs={{0,64},{8,72},{16,80},{24,88},{32,96},{40,104},{48,112},{56,120},{... | collective-permute-start | bytes 208904 | tf_op jit(solution)/shard_map/ppermute | solution.py:262
  44.7 10.6 %collective-permute-start.2 = (bf16[272,128]{1,0:T(8,128)(2,1)S(1)}, bf16[272,128]{1,0:T(8,128)(2,1)S(1)}, u32[]{:S(2)}, u32[]{:S(2)}) collective-permute-start(bf16[272,128]{1,0:T(8,128)(2,1)S(1)} %add.8), channel_id=1, source_target_pairs={{0,128},{8,136},{16,144},{24,152},{32,160},{40,168},{48,176},{56,1... | collective-permute-start | bytes 208904 | tf_op jit(solution)/shard_map/ppermute | solution.py:219
  53.5 4.1 %collective-permute-start.3 = (bf16[272,128]{1,0:T(8,128)(2,1)S(1)}, bf16[272,128]{1,0:T(8,128)(2,1)S(1)}, u32[]{:S(2)}, u32[]{:S(2)}) collective-permute-start(bf16[272,128]{1,0:T(8,128)(2,1)S(1)} %add.8), channel_id=1, source_target_pairs={{256,384},{264,392},{272,400},{280,408},{288,416},{296,424},{304,4... | collective-permute-start | bytes 208904 | tf_op jit(solution)/shard_map/ppermute | solution.py:219
  55.3 5.7 %collective-permute-start.4 = (bf16[272,128]{1,0:T(8,128)(2,1)S(1)}, bf16[272,128]{1,0:T(8,128)(2,1)S(1)}, u32[]{:S(2)}, u32[]{:S(2)}) collective-permute-start(bf16[272,128]{1,0:T(8,128)(2,1)S(1)} %add.9), channel_id=1, source_target_pairs={{128,256},{136,264},{144,272},{152,280},{160,288},{168,296},{176,3... | collective-permute-start | bytes 208904 | tf_op jit(solution)/shard_map/ppermute | solution.py:219
  61.9 3.7 %copy-start.3 = (bf16[1,128,1024]{2,1,0:T(8,128)(2,1)S(1)}, bf16[1,128,1024]{2,1,0:T(8,128)(2,1)}, u32[]{:S(2)}) copy-start(bf16[1,128,1024]{2,1,0:T(8,128)(2,1)} %param.7) | copy-start | bytes 786436
  61.9 10.9 %all-to-all-start.2 = ((bf16[8,272,128]{2,1,0:T(8,128)(2,1)}), bf16[8,272,128]{2,1,0:T(8,128)(2,1)S(1)}, u32[]{:S(2)}, u32[]{:S(2)}) async-start(bf16[8,272,128]{2,1,0:T(8,128)(2,1)} %shard_map.57), calls=%async_computation.2 | async-start | bytes 1114112 | tf_op jit(solution)/shard_map/all_to_all | solution.py:215
  65.8 0.7 copy-start.2
  74.3 9.0 %collective-permute-start.5 = (bf16[4,136,512]{2,1,0:T(8,128)(2,1)S(1)}, bf16[4,136,512]{2,1,0:T(8,128)(2,1)S(1)}, u32[]{:S(2)}, u32[]{:S(2)}) collective-permute-start(bf16[4,136,512]{2,1,0:T(8,128)(2,1)S(1)} %get-tuple-element.22), channel_id=1, source_target_pairs={{0,1},{1,0},{2,3},{3,2},{4,5},{5,4},{6,7},{7,6},{8,9},{9,8},{10,11... | collective-permute-start | bytes 1671176 | tf_op jit(solution)/shard_map/ppermute | solution.py:287
  83.4 12.0 %copy-start = (bf16[512,128]{1,0:T(8,128)(2,1)S(1)}, bf16[512,128]{1,0:T(8,128)(2,1)}, u32[]{:S(2)}) copy-start(bf16[512,128]{1,0:T(8,128)(2,1)} %hidden.1) | copy-start | bytes 393220

commit v6 on v5

--- a/solution.py
+++ b/solution.py
@@ -56,29 +56,37 @@
             yield shift, base * moved
 
 
-def project_kernel(core, own, other, gain, weights, sent, q_t, k_nat, v_t, k_t, v_diag):
-    c = core[0]
+def half_projection(part, rows, gain, weights, offset):
+    squares = jnp.zeros((128, 1), F32)
+    projected = jnp.zeros((128, 384), F32)
+    for x in (0, 2):
+        scaled, blocks = [], []
+        for block in (x, x + 1):
+            wide = part[block, rows, :].astype(F32)
+            squares += jnp.sum(wide * wide, axis=1, keepdims=True)
+            place = 2 * block + offset
+            scaled.append((wide * gain[pl.ds(place, 1), :]).astype(BF16))
+            blocks.append(jnp.concatenate([weights[kind, place] for kind in range(3)], axis=1))
+        projected += dot(jnp.concatenate(scaled, axis=1), jnp.concatenate(blocks, axis=0))
+    return squares, projected
+
+
+def own_kernel(core, own, gain, weights, squares, projected):
     for chunk in range(4):
         rows = pl.ds(128 * chunk, 128)
-        total = jnp.zeros((128, 1), F32)
-        for x in range(4):
-            for part in (own, other):
-                wide = part[x, rows, :].astype(F32)
-                total += jnp.sum(wide * wide, axis=1, keepdims=True)
-        inverse = lax.rsqrt(total / D + EPSILON)
-        projected = jnp.zeros((128, 384), F32)
-        for x in range(4):
-            first, second = 2 * x + c, 2 * x + 1 - c
-            left = (own[x, rows, :].astype(F32) * inverse * gain[pl.ds(first, 1), :]).astype(BF16)
-            right = (other[x, rows, :].astype(F32) * inverse * gain[pl.ds(second, 1), :]).astype(BF16)
-            both = jnp.concatenate(
-                [
-                    jnp.concatenate([weights[kind, block] for kind in range(3)], axis=1)
-                    for block in (first, second)
-                ],
-                axis=0,
-            )
-            projected += dot(jnp.concatenate([left, right], axis=1), both)
+        total, result = half_projection(own, rows, gain, weights, core[0])
+        squares[rows, :] = jnp.broadcast_to(total, (128, 128))
+        projected[rows, :] = result
+
+
+def project_kernel(
+    core, squares, partial, other, gain, weights, sent, q_t, k_nat, v_t, k_t, v_diag
+):
+    for chunk in range(4):
+        rows = pl.ds(128 * chunk, 128)
+        total, result = half_projection(other, rows, gain, weights, 1 - core[0])
+        inverse = lax.rsqrt((total + squares[rows, 0:1]) / D + EPSILON)
+        projected = (partial[rows, :] + result) * inverse
         rounded = projected.astype(BF16)
         k_nat[rows, :] = rounded[:, 128:256]
         values = rounded[:, 256:384]
@@ -229,6 +237,14 @@
     out_weights = w_out[0].reshape(128, 8, 128).transpose(1, 2, 0)
     own = exchange(jnp.broadcast_to(tokens, (4, T, 128)), "head", X_GROUPS)
     other = lax.ppermute(own, "head", CORE_SWAP)
+    squares, projected = call(
+        own_kernel,
+        (shape((T, 128), F32), shape((T, 384), F32)),
+        flops=T * D * 384,
+        moved=2500000,
+        in_specs=[SMEM] + [VMEM] * 3,
+        out_specs=(VMEM,) * 2,
+    )(core, own, gains, weights)
     sent, q_t, k_nat, v_t = call(
         project_kernel,
         (
@@ -240,9 +256,9 @@
         scratch=[pltpu.VMEM((128, T), F32), pltpu.VMEM((2 * T, 128), BF16)],
         flops=2 * T * D * 384 + 2 * 2112 * T * 256,
         moved=3000000,
-        in_specs=[SMEM, VMEM, VMEM, VMEM, VMEM],
+        in_specs=[SMEM] + [VMEM] * 5,
         out_specs=(VMEM,) * 4,
-    )(core, own, other, gains, weights)
+    )(core, squares, projected, other, gains, weights)
     blocks = exchange(sent, "seq", NEAR_GROUPS)
     num, den, gain = call(
         local_kernel,

time: 96.7 us -> 96.5 us (level)
  waiting for transfers between devices: 15.4 us -> 13.8 us
  starting transfers between devices: 35.6 us -> 36.7 us
    ppermute x1, starting transfers between devices: 7.42 us -> 8.56 us  [shards(): received = lax.ppermute(give, 'head', CORE_SWAP)]
    ppermute x3, waiting for transfers between devices: 4.4 us -> 3.27 us  [forward(): lax.ppermute(total, 'seq', [(WIDE * a + i, WIDE * b + i) for a, b in pair...]
where the time goes in v6:
time: 96.5 us; the launch traced here: 96 us
  starting transfers between devices  36.7 us (38%)
  blocking collectives  36.6 us (38%)
  waiting for transfers between devices  13.8 us (14%)
  Pallas kernels  6.7 us (7%)
  local copies, waits for them, and re-layouts  1.88 us (2%)
    all_to_all x3, blocking collectives, exchange(): return lax.all_to_all(blocks, axis, 0, 0, axis_index_groups=groups)  36.6 us
    ppermute x3, starting transfers between devices, forward(): lax.ppermute(total, 'seq', [(WIDE * a + i, WIDE * b + i) for a, b in pair...  11.8 us
    ppermute x1, starting transfers between devices, shards(): received = lax.ppermute(give, 'head', CORE_SWAP)  8.56 us
    ppermute x1, starting transfers between devices, shards(): other = lax.ppermute(own, 'head', CORE_SWAP)  7.78 us
    all_to_all x1, waiting for transfers between devices, exchange(): return lax.all_to_all(blocks, axis, 0, 0, axis_index_groups=groups)  5.53 us
    ppermute x1, starting transfers between devices, shards(): partner = lax.ppermute(total, 'seq', PAIR_SWAP)  4.87 us
    all_to_all x1, starting transfers between devices, exchange(): return lax.all_to_all(blocks, axis, 0, 0, axis_index_groups=groups)  3.67 us
    ppermute x3, waiting for transfers between devices, forward(): lax.ppermute(total, 'seq', [(WIDE * a + i, WIDE * b + i) for a, b in pair...  3.27 us
  transfers between devices with their start and end apart: 7, of which 6 were waited for; matrix products, arithmetic and copies ran while one was open for 0% of the time, Pallas kernels for 1%

profile of v6, /device:TPU:1, one launch (start us, length us, event | category | flops | bytes accessed | tf_op | source)
XLA Modules:
  0.0 96.0 jit_solution(14205621991116739552)
XLA Ops:
  0.0 0.0 copy-start
  0.0 1.0 %broadcast_in_dim.15 = bf16[4,512,128]{2,1,0:T(8,128)(2,1)S(1)} broadcast(bf16[512,128]{1,0:T(8,128)(2,1)} %hidden.1), dimensions={1,2} | broadcast | bytes 655360 | tf_op jit(solution)/shard_map/broadcast_in_dim | solution.py:238
  1.1 11.6 %all_to_all.20.own = bf16[4,512,128]{2,1,0:T(8,128)(2,1)S(1)} all-to-all(bf16[4,512,128]{2,1,0:T(8,128)(2,1)S(1)} %broadcast_in_dim.15), channel_id=1, replica_groups={{0,2,4,6},{1,3,5,7},{8,10,12,14},{9,11,13,15},{16,18,20,22},{17,19,21,2..., dimensions={0} | all-to-all | bytes 1048576 | tf_op jit(solution)/shard_map/all_to_all | solution.py:223
  12.6 0.0 copy-start.4
  12.6 7.8 %collective-permute-start = (bf16[4,512,128]{2,1,0:T(8,128)(2,1)S(1)}, bf16[4,512,128]{2,1,0:T(8,128)(2,1)S(1)}, u32[]{:S(2)}, u32[]{:S(2)}) collective-permute-start(bf16[4,512,128]{2,1,0:T(8,128)(2,1)S(1)} %all_to_all.20.own), channel_id=1, source_target_pairs={{0,1},{1,0},{2,3},{3,2},{4,5},{5,4},{6,7},{7,6},{8,9},{9,8},{10,11... | collective-permute-start | bytes 1572872 | tf_op jit(solution)/shard_map/ppermute | solution.py:239
  20.4 0.0 copy-done.4
  20.4 0.0 copy-done
  20.5 0.4 shard_map.55
  20.9 1.0 %collective-permute-done.other = bf16[4,512,128]{2,1,0:T(8,128)(2,1)S(1)} collective-permute-done((bf16[4,512,128]{2,1,0:T(8,128)(2,1)S(1)}, bf16[4,512,128]{2,1,0:T(8,128)(2,1)S(1)}, u32[]{:S(2)}, u32[]{:S(2)}) %collective-permute-start) | collective-permute-done | bytes 524320 | tf_op jit(solution)/shard_map/ppermute | solution.py:239
  21.9 2.0 %shard_map.56 = (bf16[8,272,128]{2,1,0:T(8,128)(2,1)S(1)}, bf16[128,512]{1,0:T(8,128)(2,1)S(1)}, bf16[512,128]{1,0:T(8,128)(2,1)S(1)}, bf16[128,512]{1,0:T(8,128)(2,1)S(1)}) custom-call(s32[1]{0:T(128)} %bitcast.core, f32[512,128]{1,0:T(8,128)S(1)} %get-tuple-element.16.squares, f32[512,384]{1,0:T(8,128)S(1)} %get-tuple-element.17.partial, ...), custom_call_target="tpu_custom_call" | custom-call | flops 956301312 | bytes 3000000 | tf_op jit(solution)/shard_map/pallas_call | solution.py:248
  23.9 13.1 %all_to_all.21.blocks = bf16[8,272,128]{2,1,0:T(8,128)(2,1)S(1)} all-to-all(bf16[8,272,128]{2,1,0:T(8,128)(2,1)S(1)} %get-tuple-element.18), channel_id=1, replica_groups={{0,8,16,24,32,40,48,56},{64,72,80,88,96,104,112,120},{128,136,144,152,1..., dimensions={0} | all-to-all | bytes 1114112 | tf_op jit(solution)/shard_map/all_to_all | solution.py:223
  37.0 0.1 shard_map.57
  37.1 4.9 %collective-permute-start.1 = (bf16[272,128]{1,0:T(8,128)(2,1)S(1)}, bf16[272,128]{1,0:T(8,128)(2,1)S(1)}, u32[]{:S(2)}, u32[]{:S(2)}) collective-permute-start(bf16[272,128]{1,0:T(8,128)(2,1)S(1)} %shard_map.57), channel_id=1, source_target_pairs={{0,64},{8,72},{16,80},{24,88},{32,96},{40,104},{48,112},{56,120},{... | collective-permute-start | bytes 208904 | tf_op jit(solution)/shard_map/ppermute | solution.py:278
  42.0 2.4 %collective-permute-done.1.partner = bf16[272,128]{1,0:T(8,128)(2,1)S(1)} collective-permute-done((bf16[272,128]{1,0:T(8,128)(2,1)S(1)}, bf16[272,128]{1,0:T(8,128)(2,1)S(1)}, u32[]{:S(2)}, u32[]{:S(2)}) %collective-permute-start.1) | collective-permute-done | bytes 69664 | tf_op jit(solution)/shard_map/ppermute | solution.py:278
  44.4 8.8 %collective-permute-start.2 = (bf16[272,128]{1,0:T(8,128)(2,1)S(1)}, bf16[272,128]{1,0:T(8,128)(2,1)S(1)}, u32[]{:S(2)}, u32[]{:S(2)}) collective-permute-start(bf16[272,128]{1,0:T(8,128)(2,1)S(1)} %add.8), channel_id=1, source_target_pairs={{0,128},{8,136},{16,144},{24,152},{32,160},{40,168},{48,176},{56,1... | collective-permute-start | bytes 208904 | tf_op jit(solution)/shard_map/ppermute | solution.py:227
  53.3 0.7 collective-permute-start.3
  53.9 1.1 %collective-permute-done.2.swapped = bf16[272,128]{1,0:T(8,128)(2,1)S(1)} collective-permute-done((bf16[272,128]{1,0:T(8,128)(2,1)S(1)}, bf16[272,128]{1,0:T(8,128)(2,1)S(1)}, u32[]{:S(2)}, u32[]{:S(2)}) %collective-permute-start.2) | collective-permute-done | bytes 69664 | tf_op jit(solution)/shard_map/ppermute | solution.py:227
  55.1 2.3 %collective-permute-start.4 = (bf16[272,128]{1,0:T(8,128)(2,1)S(1)}, bf16[272,128]{1,0:T(8,128)(2,1)S(1)}, u32[]{:S(2)}, u32[]{:S(2)}) collective-permute-start(bf16[272,128]{1,0:T(8,128)(2,1)S(1)} %add.9), channel_id=1, source_target_pairs={{128,256},{136,264},{144,272},{152,280},{160,288},{168,296},{176,3... | collective-permute-start | bytes 208904 | tf_op jit(solution)/shard_map/ppermute | solution.py:227
  57.4 0.0 collective-permute-done.3.second
  57.4 2.2 %collective-permute-done.4.third = bf16[272,128]{1,0:T(8,128)(2,1)S(1)} collective-permute-done((bf16[272,128]{1,0:T(8,128)(2,1)S(1)}, bf16[272,128]{1,0:T(8,128)(2,1)S(1)}, u32[]{:S(2)}, u32[]{:S(2)}) %collective-permute-start.4) | collective-permute-done | bytes 69664 | tf_op jit(solution)/shard_map/ppermute | solution.py:227
  59.6 0.9 shard_map.58
  60.5 0.0 copy-start.3
  60.5 3.7 %all-to-all-start.2 = ((bf16[8,272,128]{2,1,0:T(8,128)(2,1)}), bf16[8,272,128]{2,1,0:T(8,128)(2,1)S(1)}, u32[]{:S(2)}, u32[]{:S(2)}) async-start(bf16[8,272,128]{2,1,0:T(8,128)(2,1)} %shard_map.58), calls=%async_computation.2 | async-start | bytes 1114112 | tf_op jit(solution)/shard_map/all_to_all | solution.py:223
  64.2 0.0 copy-done.3
  64.2 0.2 copy.6
  64.4 0.0 copy-start.2
  64.4 0.6 copy-done.2
  65.1 0.8 shard_map.59
  65.9 5.5 %all-to-all-done.2.prefix = bf16[8,272,128]{2,1,0:T(8,128)(2,1)S(1)} async-done(((bf16[8,272,128]{2,1,0:T(8,128)(2,1)}), bf16[8,272,128]{2,1,0:T(8,128)(2,1)S(1)}, u32[]{:S(2)}, u32[]{:S(2)}) %all-to-all-start.2) | async-done | bytes 557088 | tf_op jit(solution)/shard_map/all_to_all | solution.py:223
  71.4 1.5 %shard_map.60 = (bf16[4,136,512]{2,1,0:T(8,128)(2,1)S(1)}, bf16[4,136,512]{2,1,0:T(8,128)(2,1)S(1)}) custom-call(s32[1]{0:T(128)} %bitcast.core, bf16[8,272,128]{2,1,0:T(8,128)(2,1)S(1)} %all-to-all-done.2.prefix, f32[128,512]{1,0:T(8,128)S(1)} %get-tuple-element.22.num, f32[8,512]{1,0:T(8,128)S(1)} %get-tuple-element.23.den, ...), custom_call_target="tpu_custom_call" | custom-call | flops 276824064 | bytes 2500000 | tf_op jit(solution)/shard_map/pallas_call | solution.py:294
  72.9 8.6 %collective-permute-start.5 = (bf16[4,136,512]{2,1,0:T(8,128)(2,1)S(1)}, bf16[4,136,512]{2,1,0:T(8,128)(2,1)S(1)}, u32[]{:S(2)}, u32[]{:S(2)}) collective-permute-start(bf16[4,136,512]{2,1,0:T(8,128)(2,1)S(1)} %get-tuple-element.26), channel_id=1, source_target_pairs={{0,1},{1,0},{2,3},{3,2},{4,5},{5,4},{6,7},{7,6},{8,9},{9,8},{10,11... | collective-permute-start | bytes 1671176 | tf_op jit(solution)/shard_map/ppermute | solution.py:303
  81.5 1.6 %collective-permute-done.5.received = bf16[4,136,512]{2,1,0:T(8,128)(2,1)S(1)} collective-permute-done((bf16[4,136,512]{2,1,0:T(8,128)(2,1)S(1)}, bf16[4,136,512]{2,1,0:T(8,128)(2,1)S(1)}, u32[]{:S(2)}, u32[]{:S(2)}) %collective-permute-start.5) | collective-permute-done | bytes 557088 | tf_op jit(solution)/shard_map/ppermute | solution.py:303
  83.0 0.2 shard_map.61
  83.2 0.0 copy-start.1
  83.2 12.0 %all_to_all.22.parts = bf16[4,136,512]{2,1,0:T(8,128)(2,1)S(1)} all-to-all(bf16[4,136,512]{2,1,0:T(8,128)(2,1)S(1)} %shard_map.61), channel_id=1, replica_groups={{0,2,4,6},{1,3,5,7},{8,10,12,14},{9,11,13,15},{16,18,20,22},{17,19,21,2..., dimensions={0} | all-to-all | bytes 1114112 | tf_op jit(solution)/shard_map/all_to_all | solution.py:223
  95.2 0.0 copy-done.1
  95.2 0.8 shard_map.62
  (3 shorter events, 0.0 us)
Async XLA Ops:
  0.0 20.4 %copy-start = (bf16[1,1024,3,128]{3,1,2,0:T(8,128)(2,1)S(1)}, bf16[1,1024,3,128]{3,1,2,0:T(8,128)(2,1)}, u32[]{:S(2)}) copy-start(bf16[1,1024,3,128]{3,1,2,0:T(8,128)(2,1)} %param.6) | copy-start | bytes 2359300
  12.6 7.8 %copy-start.4 = (bf16[1,1024]{1,0:T(2,128)(2,1)S(1)}, bf16[1,1024]{1,0:T(2,128)(2,1)}, u32[]{:S(2)}) copy-start(bf16[1,1024]{1,0:T(2,128)(2,1)} %param.8) | copy-start | bytes 6148
  12.6 9.3 %collective-permute-start = (bf16[4,512,128]{2,1,0:T(8,128)(2,1)S(1)}, bf16[4,512,128]{2,1,0:T(8,128)(2,1)S(1)}, u32[]{:S(2)}, u32[]{:S(2)}) collective-permute-start(bf16[4,512,128]{2,1,0:T(8,128)(2,1)S(1)} %all_to_all.20.own), channel_id=1, source_target_pairs={{0,1},{1,0},{2,3},{3,2},{4,5},{5,4},{6,7},{7,6},{8,9},{9,8},{10,11... | collective-permute-start | bytes 1572872 | tf_op jit(solution)/shard_map/ppermute | solution.py:239
  37.1 7.3 %collective-permute-start.1 = (bf16[272,128]{1,0:T(8,128)(2,1)S(1)}, bf16[272,128]{1,0:T(8,128)(2,1)S(1)}, u32[]{:S(2)}, u32[]{:S(2)}) collective-permute-start(bf16[272,128]{1,0:T(8,128)(2,1)S(1)} %shard_map.57), channel_id=1, source_target_pairs={{0,64},{8,72},{16,80},{24,88},{32,96},{40,104},{48,112},{56,120},{... | collective-permute-start | bytes 208904 | tf_op jit(solution)/shard_map/ppermute | solution.py:278
  44.4 10.6 %collective-permute-start.2 = (bf16[272,128]{1,0:T(8,128)(2,1)S(1)}, bf16[272,128]{1,0:T(8,128)(2,1)S(1)}, u32[]{:S(2)}, u32[]{:S(2)}) collective-permute-start(bf16[272,128]{1,0:T(8,128)(2,1)S(1)} %add.8), channel_id=1, source_target_pairs={{0,128},{8,136},{16,144},{24,152},{32,160},{40,168},{48,176},{56,1... | collective-permute-start | bytes 208904 | tf_op jit(solution)/shard_map/ppermute | solution.py:227
  53.3 4.1 %collective-permute-start.3 = (bf16[272,128]{1,0:T(8,128)(2,1)S(1)}, bf16[272,128]{1,0:T(8,128)(2,1)S(1)}, u32[]{:S(2)}, u32[]{:S(2)}) collective-permute-start(bf16[272,128]{1,0:T(8,128)(2,1)S(1)} %add.8), channel_id=1, source_target_pairs={{256,384},{264,392},{272,400},{280,408},{288,416},{296,424},{304,4... | collective-permute-start | bytes 208904 | tf_op jit(solution)/shard_map/ppermute | solution.py:227
  55.1 4.5 %collective-permute-start.4 = (bf16[272,128]{1,0:T(8,128)(2,1)S(1)}, bf16[272,128]{1,0:T(8,128)(2,1)S(1)}, u32[]{:S(2)}, u32[]{:S(2)}) collective-permute-start(bf16[272,128]{1,0:T(8,128)(2,1)S(1)} %add.9), channel_id=1, source_target_pairs={{128,256},{136,264},{144,272},{152,280},{160,288},{168,296},{176,3... | collective-permute-start | bytes 208904 | tf_op jit(solution)/shard_map/ppermute | solution.py:227
  60.5 3.7 %copy-start.3 = (bf16[1,128,1024]{2,1,0:T(8,128)(2,1)S(1)}, bf16[1,128,1024]{2,1,0:T(8,128)(2,1)}, u32[]{:S(2)}) copy-start(bf16[1,128,1024]{2,1,0:T(8,128)(2,1)} %param.7) | copy-start | bytes 786436
  60.5 10.9 %all-to-all-start.2 = ((bf16[8,272,128]{2,1,0:T(8,128)(2,1)}), bf16[8,272,128]{2,1,0:T(8,128)(2,1)S(1)}, u32[]{:S(2)}, u32[]{:S(2)}) async-start(bf16[8,272,128]{2,1,0:T(8,128)(2,1)} %shard_map.58), calls=%async_computation.2 | async-start | bytes 1114112 | tf_op jit(solution)/shard_map/all_to_all | solution.py:223
  64.4 0.7 copy-start.2
  72.9 10.1 %collective-permute-start.5 = (bf16[4,136,512]{2,1,0:T(8,128)(2,1)S(1)}, bf16[4,136,512]{2,1,0:T(8,128)(2,1)S(1)}, u32[]{:S(2)}, u32[]{:S(2)}) collective-permute-start(bf16[4,136,512]{2,1,0:T(8,128)(2,1)S(1)} %get-tuple-element.26), channel_id=1, source_target_pairs={{0,1},{1,0},{2,3},{3,2},{4,5},{5,4},{6,7},{7,6},{8,9},{9,8},{10,11... | collective-permute-start | bytes 1671176 | tf_op jit(solution)/shard_map/ppermute | solution.py:303
  83.2 12.0 %copy-start.1 = (bf16[512,128]{1,0:T(8,128)(2,1)S(1)}, bf16[512,128]{1,0:T(8,128)(2,1)}, u32[]{:S(2)}) copy-start(bf16[512,128]{1,0:T(8,128)(2,1)} %hidden.1) | copy-start | bytes 393220

commit v7 on v6

--- a/solution.py
+++ b/solution.py
@@ -155,7 +155,7 @@
     den[2:8, :] = jnp.zeros((6, T), F32)
 
 
-def finish_kernel(core, prefix, num, den, q_t, gain, weights, keep, give, feats):
+def finish_kernel(core, prefix, num, den, q_t, gain, weights, mixed_out, extra_out, give, feats):
     c = core[0]
     gram = jnp.concatenate([prefix[y, MAIN + EDGE :, :] for y in range(PLANE)], axis=0).astype(F32).T
     gram = gram.astype(BF16)
@@ -189,10 +189,16 @@
     ).astype(BF16)
     extra = split_rows(squares)
     for x in range(4):
-        keep[x, 0:128, :] = dot(weights[2 * x + c], mixed).astype(BF16)
         give[x, 0:128, :] = dot(weights[2 * x + 1 - c], mixed).astype(BF16)
-        keep[x, 128:136, :] = extra
         give[x, 128:136, :] = extra
+    mixed_out[...] = mixed
+    extra_out[...] = extra
+
+
+def keep_kernel(core, mixed, extra, weights, keep):
+    for x in range(4):
+        keep[x, 0:128, :] = dot(weights[2 * x + core[0]], mixed[...]).astype(BF16)
+        keep[x, 128:136, :] = extra[...]
 
 
 def split_rows(squares):
@@ -291,16 +297,24 @@
     )(odd, group, partner, *earlier, blocks)
     spread = exchange(spread, "seq", NEAR_GROUPS)
     partial = shape((4, 136, T), BF16)
-    keep, give = call(
+    mixed, extra, give = call(
         finish_kernel,
-        (partial, partial),
+        (shape((128, T), BF16), shape((8, T), BF16), partial),
         scratch=[pltpu.VMEM((2, 2112, T), BF16)],
         flops=2 * 2112 * T * 128,
         moved=2500000,
         in_specs=[SMEM] + [VMEM] * 6,
-        out_specs=(VMEM,) * 2,
+        out_specs=(VMEM,) * 3,
     )(core, spread, num, den, q_t, gain, out_weights)
     received = lax.ppermute(give, "head", CORE_SWAP)
+    keep = call(
+        keep_kernel,
+        partial,
+        flops=T * D * 128,
+        moved=900000,
+        in_specs=[SMEM] + [VMEM] * 3,
+        out_specs=VMEM,
+    )(core, mixed, extra, out_weights)
     paired = call(pair_kernel, partial, moved=1600000, in_specs=[VMEM] * 2, out_specs=VMEM)(
         keep, received
     )

time: 96.5 us -> 96.3 us (level)
  transfers between devices with their start and end apart: 7 -> 7, of which waited for: 6 -> 6; matrix products, arithmetic and copies ran while one was open for 0% -> 0% of each run, Pallas kernels for 1% -> 2%
where the time goes in v7:
time: 96.3 us; the launch traced here: 95.9 us
  starting transfers between devices  36.7 us (38%)
  blocking collectives  36.6 us (38%)
  waiting for transfers between devices  13.5 us (14%)
  Pallas kernels  6.85 us (7%)
  local copies, waits for them, and re-layouts  1.88 us (2%)
    all_to_all x3, blocking collectives, exchange(): return lax.all_to_all(blocks, axis, 0, 0, axis_index_groups=groups)  36.6 us
    ppermute x3, starting transfers between devices, forward(): lax.ppermute(total, 'seq', [(WIDE * a + i, WIDE * b + i) for a, b in pair...  11.8 us
    ppermute x1, starting transfers between devices, shards(): received = lax.ppermute(give, 'head', CORE_SWAP)  8.56 us
    ppermute x1, starting transfers between devices, shards(): other = lax.ppermute(own, 'head', CORE_SWAP)  7.78 us
    all_to_all x1, waiting for transfers between devices, exchange(): return lax.all_to_all(blocks, axis, 0, 0, axis_index_groups=groups)  5.53 us
    ppermute x1, starting transfers between devices, shards(): partner = lax.ppermute(total, 'seq', PAIR_SWAP)  4.87 us
    all_to_all x1, starting transfers between devices, exchange(): return lax.all_to_all(blocks, axis, 0, 0, axis_index_groups=groups)  3.67 us
    ppermute x3, waiting for transfers between devices, forward(): lax.ppermute(total, 'seq', [(WIDE * a + i, WIDE * b + i) for a, b in pair...  3.27 us
  transfers between devices with their start and end apart: 7, of which 6 were waited for; matrix products, arithmetic and copies ran while one was open for 0% of the time, Pallas kernels for 2%

profile of v7, /device:TPU:1, one launch (start us, length us, event | category | flops | bytes accessed | tf_op | source)
XLA Modules:
  0.0 95.9 jit_solution(15238996419766484859)
XLA Ops:
  0.0 0.0 copy-start
  0.0 1.0 %broadcast_in_dim.15 = bf16[4,512,128]{2,1,0:T(8,128)(2,1)S(1)} broadcast(bf16[512,128]{1,0:T(8,128)(2,1)} %hidden.1), dimensions={1,2} | broadcast | bytes 655360 | tf_op jit(solution)/shard_map/broadcast_in_dim | solution.py:244
  1.1 11.6 %all_to_all.20.own = bf16[4,512,128]{2,1,0:T(8,128)(2,1)S(1)} all-to-all(bf16[4,512,128]{2,1,0:T(8,128)(2,1)S(1)} %broadcast_in_dim.15), channel_id=1, replica_groups={{0,2,4,6},{1,3,5,7},{8,10,12,14},{9,11,13,15},{16,18,20,22},{17,19,21,2..., dimensions={0} | all-to-all | bytes 1048576 | tf_op jit(solution)/shard_map/all_to_all | solution.py:229
  12.6 0.0 copy-start.4
  12.6 7.8 %collective-permute-start = (bf16[4,512,128]{2,1,0:T(8,128)(2,1)S(1)}, bf16[4,512,128]{2,1,0:T(8,128)(2,1)S(1)}, u32[]{:S(2)}, u32[]{:S(2)}) collective-permute-start(bf16[4,512,128]{2,1,0:T(8,128)(2,1)S(1)} %all_to_all.20.own), channel_id=1, source_target_pairs={{0,1},{1,0},{2,3},{3,2},{4,5},{5,4},{6,7},{7,6},{8,9},{9,8},{10,11... | collective-permute-start | bytes 1572872 | tf_op jit(solution)/shard_map/ppermute | solution.py:245
  20.4 0.0 copy-done.4
  20.4 0.0 copy-done
  20.5 0.4 shard_map.55
  20.9 1.0 %collective-permute-done.other = bf16[4,512,128]{2,1,0:T(8,128)(2,1)S(1)} collective-permute-done((bf16[4,512,128]{2,1,0:T(8,128)(2,1)S(1)}, bf16[4,512,128]{2,1,0:T(8,128)(2,1)S(1)}, u32[]{:S(2)}, u32[]{:S(2)}) %collective-permute-start) | collective-permute-done | bytes 524320 | tf_op jit(solution)/shard_map/ppermute | solution.py:245
  21.9 2.0 %shard_map.56 = (bf16[8,272,128]{2,1,0:T(8,128)(2,1)S(1)}, bf16[128,512]{1,0:T(8,128)(2,1)S(1)}, bf16[512,128]{1,0:T(8,128)(2,1)S(1)}, bf16[128,512]{1,0:T(8,128)(2,1)S(1)}) custom-call(s32[1]{0:T(128)} %bitcast.core, f32[512,128]{1,0:T(8,128)S(1)} %get-tuple-element.17.squares, f32[512,384]{1,0:T(8,128)S(1)} %get-tuple-element.18.partial, ...), custom_call_target="tpu_custom_call" | custom-call | flops 956301312 | bytes 3000000 | tf_op jit(solution)/shard_map/pallas_call | solution.py:254
  23.9 13.1 %all_to_all.21.blocks = bf16[8,272,128]{2,1,0:T(8,128)(2,1)S(1)} all-to-all(bf16[8,272,128]{2,1,0:T(8,128)(2,1)S(1)} %get-tuple-element.19), channel_id=1, replica_groups={{0,8,16,24,32,40,48,56},{64,72,80,88,96,104,112,120},{128,136,144,152,1..., dimensions={0} | all-to-all | bytes 1114112 | tf_op jit(solution)/shard_map/all_to_all | solution.py:229
  37.0 0.1 shard_map.57
  37.1 4.9 %collective-permute-start.1 = (bf16[272,128]{1,0:T(8,128)(2,1)S(1)}, bf16[272,128]{1,0:T(8,128)(2,1)S(1)}, u32[]{:S(2)}, u32[]{:S(2)}) collective-permute-start(bf16[272,128]{1,0:T(8,128)(2,1)S(1)} %shard_map.57), channel_id=1, source_target_pairs={{0,64},{8,72},{16,80},{24,88},{32,96},{40,104},{48,112},{56,120},{... | collective-permute-start | bytes 208904 | tf_op jit(solution)/shard_map/ppermute | solution.py:284
  42.0 2.4 %collective-permute-done.1.partner = bf16[272,128]{1,0:T(8,128)(2,1)S(1)} collective-permute-done((bf16[272,128]{1,0:T(8,128)(2,1)S(1)}, bf16[272,128]{1,0:T(8,128)(2,1)S(1)}, u32[]{:S(2)}, u32[]{:S(2)}) %collective-permute-start.1) | collective-permute-done | bytes 69664 | tf_op jit(solution)/shard_map/ppermute | solution.py:284
  44.4 8.8 %collective-permute-start.2 = (bf16[272,128]{1,0:T(8,128)(2,1)S(1)}, bf16[272,128]{1,0:T(8,128)(2,1)S(1)}, u32[]{:S(2)}, u32[]{:S(2)}) collective-permute-start(bf16[272,128]{1,0:T(8,128)(2,1)S(1)} %add.8), channel_id=1, source_target_pairs={{0,128},{8,136},{16,144},{24,152},{32,160},{40,168},{48,176},{56,1... | collective-permute-start | bytes 208904 | tf_op jit(solution)/shard_map/ppermute | solution.py:233
  53.3 0.7 collective-permute-start.3
  53.9 1.1 %collective-permute-done.2.swapped = bf16[272,128]{1,0:T(8,128)(2,1)S(1)} collective-permute-done((bf16[272,128]{1,0:T(8,128)(2,1)S(1)}, bf16[272,128]{1,0:T(8,128)(2,1)S(1)}, u32[]{:S(2)}, u32[]{:S(2)}) %collective-permute-start.2) | collective-permute-done | bytes 69664 | tf_op jit(solution)/shard_map/ppermute | solution.py:233
  55.1 2.3 %collective-permute-start.4 = (bf16[272,128]{1,0:T(8,128)(2,1)S(1)}, bf16[272,128]{1,0:T(8,128)(2,1)S(1)}, u32[]{:S(2)}, u32[]{:S(2)}) collective-permute-start(bf16[272,128]{1,0:T(8,128)(2,1)S(1)} %add.9), channel_id=1, source_target_pairs={{128,256},{136,264},{144,272},{152,280},{160,288},{168,296},{176,3... | collective-permute-start | bytes 208904 | tf_op jit(solution)/shard_map/ppermute | solution.py:233
  57.4 0.0 collective-permute-done.3.second
  57.4 2.2 %collective-permute-done.4.third = bf16[272,128]{1,0:T(8,128)(2,1)S(1)} collective-permute-done((bf16[272,128]{1,0:T(8,128)(2,1)S(1)}, bf16[272,128]{1,0:T(8,128)(2,1)S(1)}, u32[]{:S(2)}, u32[]{:S(2)}) %collective-permute-start.4) | collective-permute-done | bytes 69664 | tf_op jit(solution)/shard_map/ppermute | solution.py:233
  59.6 0.9 shard_map.58
  60.5 0.0 copy-start.3
  60.5 3.7 %all-to-all-start.2 = ((bf16[8,272,128]{2,1,0:T(8,128)(2,1)}), bf16[8,272,128]{2,1,0:T(8,128)(2,1)S(1)}, u32[]{:S(2)}, u32[]{:S(2)}) async-start(bf16[8,272,128]{2,1,0:T(8,128)(2,1)} %shard_map.58), calls=%async_computation.2 | async-start | bytes 1114112 | tf_op jit(solution)/shard_map/all_to_all | solution.py:229
  64.2 0.0 copy-done.3
  64.2 0.2 copy.6
  64.4 0.0 copy-start.2
  64.4 0.6 copy-done.2
  65.1 0.8 shard_map.59
  65.9 5.5 %all-to-all-done.2.prefix = bf16[8,272,128]{2,1,0:T(8,128)(2,1)S(1)} async-done(((bf16[8,272,128]{2,1,0:T(8,128)(2,1)}), bf16[8,272,128]{2,1,0:T(8,128)(2,1)S(1)}, u32[]{:S(2)}, u32[]{:S(2)}) %all-to-all-start.2) | async-done | bytes 557088 | tf_op jit(solution)/shard_map/all_to_all | solution.py:229
  71.4 1.4 %shard_map.60 = (bf16[128,512]{1,0:T(8,128)(2,1)S(1)}, bf16[8,512]{1,0:T(8,128)(2,1)S(1)}, bf16[4,136,512]{2,1,0:T(8,128)(2,1)S(1)}) custom-call(s32[1]{0:T(128)} %bitcast.core, bf16[8,272,128]{2,1,0:T(8,128)(2,1)S(1)} %all-to-all-done.2.prefix, f32[128,512]{1,0:T(8,128)S(1)} %get-tuple-element.23.num, f32[8,512]{1,0:T(8,128)S(1)} %get-tuple-element.24.den, ...), custom_call_target="tpu_custom_call" | custom-call | flops 276824064 | bytes 2500000 | tf_op jit(solution)/shard_map/pallas_call | solution.py:300
  72.8 8.6 %collective-permute-start.5 = (bf16[4,136,512]{2,1,0:T(8,128)(2,1)S(1)}, bf16[4,136,512]{2,1,0:T(8,128)(2,1)S(1)}, u32[]{:S(2)}, u32[]{:S(2)}) collective-permute-start(bf16[4,136,512]{2,1,0:T(8,128)(2,1)S(1)} %get-tuple-element.28), channel_id=1, source_target_pairs={{0,1},{1,0},{2,3},{3,2},{4,5},{5,4},{6,7},{7,6},{8,9},{9,8},{10,11... | collective-permute-start | bytes 1671176 | tf_op jit(solution)/shard_map/ppermute | solution.py:309
  81.3 0.3 shard_map.61.keep
  81.6 1.3 %collective-permute-done.5.received = bf16[4,136,512]{2,1,0:T(8,128)(2,1)S(1)} collective-permute-done((bf16[4,136,512]{2,1,0:T(8,128)(2,1)S(1)}, bf16[4,136,512]{2,1,0:T(8,128)(2,1)S(1)}, u32[]{:S(2)}, u32[]{:S(2)}) %collective-permute-start.5) | collective-permute-done | bytes 557088 | tf_op jit(solution)/shard_map/ppermute | solution.py:309
  82.9 0.2 shard_map.62
  83.1 0.0 copy-start.1
  83.1 12.0 %all_to_all.22.parts = bf16[4,136,512]{2,1,0:T(8,128)(2,1)S(1)} all-to-all(bf16[4,136,512]{2,1,0:T(8,128)(2,1)S(1)} %shard_map.62), channel_id=1, replica_groups={{0,2,4,6},{1,3,5,7},{8,10,12,14},{9,11,13,15},{16,18,20,22},{17,19,21,2..., dimensions={0} | all-to-all | bytes 1114112 | tf_op jit(solution)/shard_map/all_to_all | solution.py:229
  95.0 0.0 copy-done.1
  95.0 0.8 shard_map.63
  (3 shorter events, 0.0 us)
Async XLA Ops:
  0.0 20.4 %copy-start = (bf16[1,1024,3,128]{3,1,2,0:T(8,128)(2,1)S(1)}, bf16[1,1024,3,128]{3,1,2,0:T(8,128)(2,1)}, u32[]{:S(2)}) copy-start(bf16[1,1024,3,128]{3,1,2,0:T(8,128)(2,1)} %param.6) | copy-start | bytes 2359300
  12.6 7.8 %copy-start.4 = (bf16[1,1024]{1,0:T(2,128)(2,1)S(1)}, bf16[1,1024]{1,0:T(2,128)(2,1)}, u32[]{:S(2)}) copy-start(bf16[1,1024]{1,0:T(2,128)(2,1)} %param.8) | copy-start | bytes 6148
  12.6 9.3 %collective-permute-start = (bf16[4,512,128]{2,1,0:T(8,128)(2,1)S(1)}, bf16[4,512,128]{2,1,0:T(8,128)(2,1)S(1)}, u32[]{:S(2)}, u32[]{:S(2)}) collective-permute-start(bf16[4,512,128]{2,1,0:T(8,128)(2,1)S(1)} %all_to_all.20.own), channel_id=1, source_target_pairs={{0,1},{1,0},{2,3},{3,2},{4,5},{5,4},{6,7},{7,6},{8,9},{9,8},{10,11... | collective-permute-start | bytes 1572872 | tf_op jit(solution)/shard_map/ppermute | solution.py:245
  37.1 7.3 %collective-permute-start.1 = (bf16[272,128]{1,0:T(8,128)(2,1)S(1)}, bf16[272,128]{1,0:T(8,128)(2,1)S(1)}, u32[]{:S(2)}, u32[]{:S(2)}) collective-permute-start(bf16[272,128]{1,0:T(8,128)(2,1)S(1)} %shard_map.57), channel_id=1, source_target_pairs={{0,64},{8,72},{16,80},{24,88},{32,96},{40,104},{48,112},{56,120},{... | collective-permute-start | bytes 208904 | tf_op jit(solution)/shard_map/ppermute | solution.py:284
  44.4 10.6 %collective-permute-start.2 = (bf16[272,128]{1,0:T(8,128)(2,1)S(1)}, bf16[272,128]{1,0:T(8,128)(2,1)S(1)}, u32[]{:S(2)}, u32[]{:S(2)}) collective-permute-start(bf16[272,128]{1,0:T(8,128)(2,1)S(1)} %add.8), channel_id=1, source_target_pairs={{0,128},{8,136},{16,144},{24,152},{32,160},{40,168},{48,176},{56,1... | collective-permute-start | bytes 208904 | tf_op jit(solution)/shard_map/ppermute | solution.py:233
  53.3 4.1 %collective-permute-start.3 = (bf16[272,128]{1,0:T(8,128)(2,1)S(1)}, bf16[272,128]{1,0:T(8,128)(2,1)S(1)}, u32[]{:S(2)}, u32[]{:S(2)}) collective-permute-start(bf16[272,128]{1,0:T(8,128)(2,1)S(1)} %add.8), channel_id=1, source_target_pairs={{256,384},{264,392},{272,400},{280,408},{288,416},{296,424},{304,4... | collective-permute-start | bytes 208904 | tf_op jit(solution)/shard_map/ppermute | solution.py:233
  55.1 4.5 %collective-permute-start.4 = (bf16[272,128]{1,0:T(8,128)(2,1)S(1)}, bf16[272,128]{1,0:T(8,128)(2,1)S(1)}, u32[]{:S(2)}, u32[]{:S(2)}) collective-permute-start(bf16[272,128]{1,0:T(8,128)(2,1)S(1)} %add.9), channel_id=1, source_target_pairs={{128,256},{136,264},{144,272},{152,280},{160,288},{168,296},{176,3... | collective-permute-start | bytes 208904 | tf_op jit(solution)/shard_map/ppermute | solution.py:233
  60.5 3.7 %copy-start.3 = (bf16[1,128,1024]{2,1,0:T(8,128)(2,1)S(1)}, bf16[1,128,1024]{2,1,0:T(8,128)(2,1)}, u32[]{:S(2)}) copy-start(bf16[1,128,1024]{2,1,0:T(8,128)(2,1)} %param.7) | copy-start | bytes 786436
  60.5 10.9 %all-to-all-start.2 = ((bf16[8,272,128]{2,1,0:T(8,128)(2,1)}), bf16[8,272,128]{2,1,0:T(8,128)(2,1)S(1)}, u32[]{:S(2)}, u32[]{:S(2)}) async-start(bf16[8,272,128]{2,1,0:T(8,128)(2,1)} %shard_map.58), calls=%async_computation.2 | async-start | bytes 1114112 | tf_op jit(solution)/shard_map/all_to_all | solution.py:229
  64.4 0.7 copy-start.2
  72.8 10.1 %collective-permute-start.5 = (bf16[4,136,512]{2,1,0:T(8,128)(2,1)S(1)}, bf16[4,136,512]{2,1,0:T(8,128)(2,1)S(1)}, u32[]{:S(2)}, u32[]{:S(2)}) collective-permute-start(bf16[4,136,512]{2,1,0:T(8,128)(2,1)S(1)} %get-tuple-element.28), channel_id=1, source_target_pairs={{0,1},{1,0},{2,3},{3,2},{4,5},{5,4},{6,7},{7,6},{8,9},{9,8},{10,11... | collective-permute-start | bytes 1671176 | tf_op jit(solution)/shard_map/ppermute | solution.py:309
  83.1 12.0 %copy-start.1 = (bf16[512,128]{1,0:T(8,128)(2,1)S(1)}, bf16[512,128]{1,0:T(8,128)(2,1)}, u32[]{:S(2)}) copy-start(bf16[512,128]{1,0:T(8,128)(2,1)} %hidden.1) | copy-start | bytes 393220
